TPU v7x, 32 devices: a whole 2x2x4 slice. The times are simulated.
32 devices in a mesh: seq: 16 (over z, x, core), batch: 2 (over y).
Axes of the slice: x: 2, y: 2, z: 4, core: 2. Of those that a mesh axis runs over, the one named last changes fastest.
Arguments:
- inputs: bfloat16 [2, 4096, 768], P('batch', 'seq'), may hold values from -6 to 6
- lengths: int32 [2], P('batch'), may hold values from 1024 to 4096, as said below
- cotangent: bfloat16 [2, 4096, 768], P('batch', 'seq'), may hold values from -6 to 6
- triple_weight: float32 [768, 2304], P(('seq', 'batch')), may hold values from -0.3125 to 0.3125
- query_bias: float32 [768], P(('seq', 'batch')), may hold values from -3 to 3
- value_bias: float32 [768], P(('seq', 'batch')), may hold values from -3 to 3
- output_weight: float32 [768, 768], P(('seq', 'batch')), may hold values from -1.75 to 1.75
- output_bias: float32 [768], P(('seq', 'batch')), may hold values from -3 to 3
- first_gain: float32 [768], P(('seq', 'batch')), may hold values from 0.5 to 1.5
- first_shift: float32 [768], P(('seq', 'batch')), may hold values from -3 to 3
- expand_weight: float32 [768, 3072], P(('seq', 'batch')), may hold values from -0.21875 to 0.21875
- expand_bias: float32 [3072], P(('seq', 'batch')), may hold values from -3 to 3
- shrink_weight: float32 [3072, 768], P(('seq', 'batch')), may hold values from -0.109375 to 0.109375
- shrink_bias: float32 [768], P(('seq', 'batch')), may hold values from -3 to 3
- second_gain: float32 [768], P(('seq', 'batch')), may hold values from 0.5 to 1.5
- second_shift: float32 [768], P(('seq', 'batch')), may hold values from -3 to 3
Outputs:
- output: bfloat16 [2, 4096, 768], P('batch', 'seq')
- input_grad: bfloat16 [2, 4096, 768], P('batch', 'seq')
- grad_triple_weight: float32 [768, 2304], P(('seq', 'batch'))
- grad_query_bias: float32 [768], P(('seq', 'batch'))
- grad_value_bias: float32 [768], P(('seq', 'batch'))
- grad_output_weight: float32 [768, 768], P(('seq', 'batch'))
- grad_output_bias: float32 [768], P(('seq', 'batch'))
- grad_first_gain: float32 [768], P(('seq', 'batch'))
- grad_first_shift: float32 [768], P(('seq', 'batch'))
- grad_expand_weight: float32 [768, 3072], P(('seq', 'batch'))
- grad_expand_bias: float32 [3072], P(('seq', 'batch'))
- grad_shrink_weight: float32 [3072, 768], P(('seq', 'batch'))
- grad_shrink_bias: float32 [768], P(('seq', 'batch'))
- grad_second_gain: float32 [768], P(('seq', 'batch'))
- grad_second_shift: float32 [768], P(('seq', 'batch'))
Inputs may be any that keep to these rules, and one draw needn't show every extreme that they name: The first lengths slots of a sequence hold its tokens, the others are padding; in every draw some sequence fills all 4096 slots.
All inputs are finite; a program needn't handle non-finite values.
Results may differ from a plain program's by a relative error of at most 0.019.
The roundings to bfloat16 on the way count: a program that leaves them out, or rounds other values in their place, can miss the bound.
Values may be sent and summed in bfloat16 or wider, within the bound.
No kernel may reach another device: no remote copies, remote signals or barrier semaphores. Data moves between devices by JAX's collectives and lax.ppermute only.
A program may use at most 192 MiB of HBM per device.

v0:
```python
from functools import partial
import math

import jax
import jax.numpy as jnp
from jax import lax
from jax.experimental import pallas as pl
from jax.experimental.pallas import tpu as pltpu
from jax.sharding import Mesh, PartitionSpec as P

HEADS = 12
HEAD_DIM = 64
GROUPS = 4
OWN_HEADS = HEADS // GROUPS
OWN_WIDTH = OWN_HEADS * HEAD_DIM
LANES = 128
WIDE = 640
VECTORS = 3 * OWN_WIDTH

bf16 = jnp.bfloat16
f32 = jnp.float32
masked_score = -1e30
norm_eps = 1e-12
log2_e = 1.4426950408889634
CONTRACT_LAST = (((1,), (1,)), ((), ()))
MIB = 1024 * 1024
AXES = ("q", "x", "c", "b")


def split_three(value):
    high = value.astype(bf16).astype(f32)
    rest = value - high
    mid = rest.astype(bf16).astype(f32)
    low = (rest - mid).astype(bf16).astype(f32)
    return high, mid, low


def low_half(tile, lane, from_high):
    turned = pltpu.roll(tile, HEAD_DIM, 1)
    low = lane < HEAD_DIM
    return jnp.where(low, turned, tile) if from_high else jnp.where(low, tile, turned)


def place_of(kind, h):
    slot = kind * OWN_HEADS + h
    return slot // 2, slot % 2


def forward_kernel(first, last, block_q, block_k, *refs):
    refs = list(refs)
    where_ref = refs.pop(0)
    far = [refs.pop(0) for _ in range(5)]
    bias_ref = refs.pop(0)
    if not first:
        qx_ref, peak_in, sum_in = [refs.pop(0) for _ in range(3)]
    kept = [refs.pop(0) for _ in range(2)]
    if first:
        qx_ref, qp_ref = [refs.pop(0) for _ in range(2)]
    if last:
        att_refs = [refs.pop(0) for _ in range(4)]
        attx_ref, qx2_ref = [refs.pop(0) for _ in range(2)]
    else:
        peak_out, sum_out = [refs.pop(0) for _ in range(2)]
    vt_ref, kx_ref, vx_ref, sem, *near = refs
    loads = [pltpu.make_async_copy(f, n, sem.at[2 + i]) for i, (f, n) in enumerate(zip(far, near))]
    for i in (4, 0, 1, 2, 3):
        loads[i].start()
    *pieces, w_ref = near
    stores = [
        pltpu.make_async_copy(kx_ref, kept[0], sem.at[0]),
        pltpu.make_async_copy(vx_ref, kept[1], sem.at[1]),
    ]
    piece_rows = pieces[0].shape[0]
    rows_in = 4 * piece_rows
    lane = lax.broadcasted_iota(jnp.int32, (piece_rows, LANES), 1)
    row = lax.broadcasted_iota(jnp.int32, (piece_rows, LANES), 0)
    low = lane < HEAD_DIM
    length = where_ref[4]
    three = (lane >= HEAD_DIM) & (lane < HEAD_DIM + 3)
    skip = 0 if first else LANES
    for p in range(4):
        rows = slice(p * piece_rows, (p + 1) * piece_rows)
        if p == 0:
            loads[4].wait()
        loads[p].wait()
        joint = jnp.dot(pieces[p][...], w_ref[:, skip:], preferred_element_type=f32)
        joint = joint + bias_ref[:, skip:]
        bias = jnp.where(where_ref[p] + row < length, 0.0, masked_score)
        key_extra = jnp.where(three, 1.0, jnp.where(lane == HEAD_DIM + 3, bias, 0.0))

        def head_of(kind, h):
            tile, high = place_of(kind, h)
            return low_half(joint[:, tile * LANES - skip : (tile + 1) * LANES - skip], lane, high)

        for h in range(OWN_HEADS):
            k = head_of(1, h)
            kx_ref[h, rows, :LANES] = k.astype(bf16)
            kx_ref[h, rows, LANES:] = jnp.where(low, k, key_extra).astype(bf16)
            v = jnp.where(low, head_of(2, h), 0.0)
            vx_ref[h, rows, :] = jnp.where(three, -1.0, v).astype(bf16)
            vt = jnp.where(lane == HEAD_DIM, 1.0, v).T
            vt_ref[h, :, rows] = vt[:80].astype(bf16)
            if first:
                q = head_of(0, h).astype(bf16).astype(f32)
                qp_ref[h, rows, :] = jnp.where(low, q, 0.0).astype(bf16)
                high, mid, rest = split_three(q * (HEAD_DIM**-0.5 * log2_e))
                qx_ref[h, rows, :LANES] = jnp.where(low, high, mid).astype(bf16)
                one = jnp.where(lane == HEAD_DIM + 3, 1.0, 0.0)
                qx_ref[h, rows, LANES:] = jnp.where(low, rest, one).astype(bf16)
    for store in stores:
        store.start()
    for h in range(OWN_HEADS):
        for i in range(rows_in // block_q):
            cols = slice(i * block_q, (i + 1) * block_q)
            q = qx_ref[h, cols, :]
            if first:
                peak = jnp.full((1, block_q), masked_score, f32)
                total = jnp.zeros((80, block_q), f32)
            else:
                peak = peak_in[h, :1, cols]
                total = sum_in[h, :, cols]
            for j in range(rows_in // block_k):
                ks = slice(j * block_k, (j + 1) * block_k)
                s = lax.dot_general(kx_ref[h, ks, :], q, CONTRACT_LAST, preferred_element_type=f32)
                new_peak = jnp.maximum(peak, jnp.max(s, axis=0, keepdims=True))
                prob = jnp.exp2(s - new_peak).astype(bf16)
                total = total * jnp.exp2(peak - new_peak) + jnp.dot(
                    vt_ref[h, :, ks], prob, preferred_element_type=f32
                )
                peak = new_peak
            if last:
                denom = total[HEAD_DIM : HEAD_DIM + 1]
                n_high, n_mid, n_low = split_three(-(peak + jnp.log2(denom)))
                tall = jnp.concatenate(
                    [
                        total[:HEAD_DIM] / denom,
                        n_high,
                        n_mid,
                        n_low,
                        jnp.zeros((HEAD_DIM - 3, block_q), f32),
                    ],
                    axis=0,
                )
                attx_ref[h, cols, :] = tall.T
            else:
                peak_out[h, :, cols] = jnp.broadcast_to(peak, (8, block_q))
                sum_out[h, :, cols] = total
    if last:
        for p in range(4):
            rows = slice(p * piece_rows, (p + 1) * piece_rows)
            heads = [attx_ref[h, rows, :] for h in range(OWN_HEADS)]
            pair = jnp.where(low, heads[0], pltpu.roll(heads[1], HEAD_DIM, 1))
            att_refs[p][:, :LANES] = pair.astype(bf16)
            att_refs[p][:, LANES:] = heads[2][:, :HEAD_DIM].astype(bf16)
            for h in range(OWN_HEADS):
                qx2_ref[h, rows, :LANES] = qx_ref[h, rows, :LANES]
                old = qx_ref[h, rows, LANES:].astype(f32)
                qx2_ref[h, rows, LANES:] = jnp.where(three, heads[h], old).astype(bf16)
    for store in stores:
        store.wait()


def in_hbm(value):
    return pltpu.with_memory_space_constraint(value, pltpu.HBM)


def vmem_specs(n):
    return [pl.BlockSpec(memory_space=pltpu.VMEM) for _ in range(n)]


def attend_chunk(first, last, where, pieces, weights, carry):
    piece_rows = pieces[0].shape[0]
    rows = 4 * piece_rows
    w, bias_row = weights
    far = [in_hbm(v) for v in (*pieces, w)]
    operands = [where, *far, bias_row]
    operands += [] if first else list(carry)
    wide_keys = jax.ShapeDtypeStruct((OWN_HEADS, rows, 2 * LANES), bf16)
    out_shape = [pltpu.HBM(wide_keys.shape, bf16), pltpu.HBM((OWN_HEADS, rows, LANES), bf16)]
    if first:
        out_shape += [wide_keys, jax.ShapeDtypeStruct((OWN_HEADS, rows, LANES), bf16)]
    if last:
        out_shape += [jax.ShapeDtypeStruct((piece_rows, OWN_WIDTH), bf16)] * 4
        out_shape += [jax.ShapeDtypeStruct((OWN_HEADS, rows, LANES), f32), wide_keys]
    else:
        out_shape += [
            jax.ShapeDtypeStruct((OWN_HEADS, 8, rows), f32),
            jax.ShapeDtypeStruct((OWN_HEADS, 80, rows), f32),
        ]
    return pl.pallas_call(
        partial(forward_kernel, first, last, min(1024, rows), min(1024, rows)),
        out_shape=out_shape,
        in_specs=[pl.BlockSpec(memory_space=pltpu.SMEM)]
        + [pl.BlockSpec(memory_space=pltpu.HBM)] * len(far)
        + vmem_specs(len(operands) - 1 - len(far)),
        out_specs=[pl.BlockSpec(memory_space=pltpu.HBM)] * 2 + vmem_specs(len(out_shape) - 2),
        scratch_shapes=[
            pltpu.VMEM((OWN_HEADS, 80, rows), bf16),
            pltpu.VMEM((OWN_HEADS, rows, 2 * LANES), bf16),
            pltpu.VMEM((OWN_HEADS, rows, LANES), bf16),
            pltpu.SemaphoreType.DMA((7,)),
            *[pltpu.VMEM(v.shape, v.dtype) for v in (*pieces, w)],
        ],
        compiler_params=pltpu.CompilerParams(vmem_limit_bytes=20 * MIB),
        cost_estimate=pl.CostEstimate(
            flops=int(8e9), transcendentals=OWN_HEADS * rows * rows, bytes_accessed=int(1e7)
        ),
        name="attend_forward",
    )(*operands)


def backward_kernel(first, last, block_q, block_k, *refs):
    refs = list(refs)
    far = [refs.pop(0) for _ in range(7)]
    qx_ref, qp_ref = [refs.pop(0) for _ in range(2)]
    if first:
        grads = [refs.pop(0) for _ in range(4)]
        attx_ref = refs.pop(0)
    else:
        dox_ref, dqt_in, dw_in, col_in = [refs.pop(0) for _ in range(4)]
    keep_ref, send_ref = [refs.pop(0) for _ in range(2)]
    if first:
        dox_ref = refs.pop(0)
    if last:
        dw_out, col_out = [refs.pop(0) for _ in range(2)]
        dqt_ref = refs.pop()
    else:
        dqt_ref, dw_out, col_out = [refs.pop(0) for _ in range(3)]
    kt_ref, all_ref, sem = refs[:3]
    near = refs[3:]
    kx_ref, vx_ref, w_ref, *pieces = near
    loads = []
    for f, n in zip(far[:2], near[:2]):
        loads += [(f.at[h], n.at[h]) for h in range(OWN_HEADS)]
    loads += list(zip(far[2:], near[2:]))
    loads = [pltpu.make_async_copy(f, n, sem.at[i]) for i, (f, n) in enumerate(loads)]
    for i in (0, OWN_HEADS, *range(1, OWN_HEADS), *range(OWN_HEADS + 1, len(loads))):
        loads[i].start()
    rows_in = kx_ref.shape[1]
    piece_rows = rows_in // 4
    scale = HEAD_DIM**-0.5
    lane = lax.broadcasted_iota(jnp.int32, (piece_rows, LANES), 1)
    if first:
        for p in range(4):
            rows = slice(p * piece_rows, (p + 1) * piece_rows)
            left = grads[p][:, :LANES].astype(f32)
            right = grads[p][:, LANES:].astype(f32)
            right = jnp.concatenate([right, jnp.zeros_like(right)], axis=1)
            for h, wide in enumerate((left, pltpu.roll(left, HEAD_DIM, 1), right)):
                grad = jnp.where(lane < HEAD_DIM, wide, 0.0)
                delta = jnp.sum(grad * attx_ref[h, rows, :], axis=1, keepdims=True)
                d_high, d_mid, d_low = split_three(delta)
                grad = jnp.where(lane == HEAD_DIM, d_high, grad)
                grad = jnp.where(lane == HEAD_DIM + 1, d_mid, grad)
                grad = jnp.where(lane == HEAD_DIM + 2, d_low, grad)
                dox_ref[h, rows, :] = grad.astype(bf16)
        dqt_ref[...] = jnp.zeros_like(dqt_ref)
    else:
        dqt_ref[...] = dqt_in[...]
    lane_k = lax.broadcasted_iota(jnp.int32, (block_k, LANES), 1)
    low_k = lane_k < HEAD_DIM
    for j in range(rows_in // block_k):
        ks = slice(j * block_k, (j + 1) * block_k)
        parts = {}
        for h in range(OWN_HEADS):
            if j == 0:
                loads[h].wait()
                loads[OWN_HEADS + h].wait()
                kt_ref[h] = kx_ref[h, :, LANES:].astype(f32).T[:HEAD_DIM].astype(bf16)
            k = kx_ref[h, ks, :]
            v = vx_ref[h, ks, :]
            kt = kt_ref[h, :, ks]
            dk = jnp.zeros((block_k, LANES), f32)
            dv = jnp.zeros((block_k, LANES), f32)
            for i in range(rows_in // block_q):
                qs = slice(i * block_q, (i + 1) * block_q)
                s = lax.dot_general(k, qx_ref[h, qs, :], CONTRACT_LAST, preferred_element_type=f32)
                prob = jnp.exp2(s)
                do = dox_ref[h, qs, :]
                dp = lax.dot_general(v, do, CONTRACT_LAST, preferred_element_type=f32)
                ds = (prob * dp).astype(bf16)
                dv = dv + jnp.dot(prob.astype(bf16), do, preferred_element_type=f32)
                dk = dk + jnp.dot(ds, qp_ref[h, qs, :], preferred_element_type=f32)
                dqt_ref[h, :, qs] += jnp.dot(kt, ds, preferred_element_type=f32)
            parts[OWN_HEADS + h] = dk * scale
            parts[2 * OWN_HEADS + h] = dv
        for tile in range(1, WIDE // LANES):
            left, right = parts.get(2 * tile), parts.get(2 * tile + 1)
            left = jnp.zeros((block_k, LANES), f32) if left is None else left
            right = 0.0 if right is None else pltpu.roll(right, HEAD_DIM, 1)
            both = jnp.where(low_k, left, right).astype(bf16)
            all_ref[ks, tile * LANES : (tile + 1) * LANES] = both
    if last:
        tall = jnp.concatenate([dqt_ref[0], dqt_ref[1]], axis=0) * scale
        all_ref[:, :LANES] = tall.T.astype(bf16)
        tall = dqt_ref[2] * scale
        tall = jnp.concatenate([tall, jnp.zeros_like(tall)], axis=0).T
        lane_all = lax.broadcasted_iota(jnp.int32, (rows_in, LANES), 1)
        old = all_ref[:, LANES : 2 * LANES].astype(f32)
        all_ref[:, LANES : 2 * LANES] = jnp.where(lane_all < HEAD_DIM, tall, old).astype(bf16)
    skip = 0 if last else LANES
    for load in loads[2 * OWN_HEADS :]:
        load.wait()
    d_weight = [None, None]
    for p in range(4):
        rows = slice(p * piece_rows, (p + 1) * piece_rows)
        own = all_ref[rows, skip:]
        dx = lax.dot_general(own, w_ref[:, skip:], CONTRACT_LAST, preferred_element_type=f32)
        out_ref = keep_ref if p % 2 == 0 else send_ref
        out_ref[p // 2] = dx.astype(bf16)
        piece = lax.dot_general(
            pieces[p][...], own, (((0,), (0,)), ((), ())), preferred_element_type=f32
        )
        d_weight[0] = piece if p == 0 else d_weight[0] + piece
        col = jnp.sum(own.astype(f32), axis=0, keepdims=True)
        d_weight[1] = col if p == 0 else d_weight[1] + col
    grad, col = d_weight
    if last:
        dw_out[:, :LANES] = grad[:, :LANES].astype(bf16)
        dw_out[:, LANES:] = (grad[:, LANES:] + dw_in[...]).astype(bf16)
        col_out[:, :LANES] = jnp.broadcast_to(col[:, :LANES], (8, LANES))
        col_out[:, LANES:] = col[:, LANES:] + col_in[...]
    elif first:
        dw_out[...] = grad
        col_out[...] = jnp.broadcast_to(col, col_out.shape)
    else:
        dw_out[...] = grad + dw_in[...]
        col_out[...] = col + col_in[...]


def attend_back_chunk(first, last, chunk, pieces, shared, carry):
    kx, vx = chunk
    qx2, qp, w, grads, attx = shared
    rows, width = kx.shape[1], w.shape[0]
    far = [in_hbm(v) for v in (kx, vx, w, *pieces)]
    operands = [*far, qx2, qp]
    operands += [*grads, attx] if first else list(carry)
    half = jax.ShapeDtypeStruct((2, rows // 4, width), bf16)
    out_shape = [half, half]
    scratch = [
        pltpu.VMEM((OWN_HEADS, HEAD_DIM, rows), bf16),
        pltpu.VMEM((rows, WIDE), bf16),
        pltpu.SemaphoreType.DMA((2 * OWN_HEADS + 5,)),
        *[pltpu.VMEM(v.shape, v.dtype) for v in far],
    ]
    if first:
        out_shape.append(jax.ShapeDtypeStruct((OWN_HEADS, rows, LANES), bf16))
    if last:
        out_shape.append(jax.ShapeDtypeStruct((width, WIDE), bf16))
        out_shape.append(jax.ShapeDtypeStruct((8, WIDE), f32))
        scratch.append(pltpu.VMEM((OWN_HEADS, HEAD_DIM, rows), f32))
    else:
        out_shape.append(jax.ShapeDtypeStruct((OWN_HEADS, HEAD_DIM, rows), f32))
        out_shape.append(jax.ShapeDtypeStruct((width, WIDE - LANES), f32))
        out_shape.append(jax.ShapeDtypeStruct((8, WIDE - LANES), f32))
    return pl.pallas_call(
        partial(backward_kernel, first, last, min(256, rows), min(1024, rows)),
        out_shape=out_shape,
        in_specs=[pl.BlockSpec(memory_space=pltpu.HBM)] * len(far)
        + vmem_specs(len(operands) - len(far)),
        out_specs=vmem_specs(len(out_shape)),
        scratch_shapes=scratch,
        compiler_params=pltpu.CompilerParams(vmem_limit_bytes=26 * MIB),
        cost_estimate=pl.CostEstimate(
            flops=int(1.5e10), transcendentals=OWN_HEADS * rows * rows, bytes_accessed=int(1e7)
        ),
        name="attend_backward",
    )(*operands)


def norm_forward(value, gain, shift):
    center = value - jnp.mean(value, axis=-1, keepdims=True)
    spread = jnp.mean(center * center, axis=-1, keepdims=True)
    inverse = lax.rsqrt(spread + norm_eps)
    normal = center * inverse
    return normal * gain + shift, normal, inverse


def norm_backward(grad, gain, normal, inverse):
    inner = grad * gain
    mean = jnp.mean(inner, axis=-1, keepdims=True)
    along = jnp.mean(inner * normal, axis=-1, keepdims=True)
    return inverse * (inner - mean - normal * along)


CONTRACT_FIRST = (((0,), (0,)), ((), ()))


def ffn_kernel(layout, *refs):
    n_q, n_b, own_rows, fold, aligned = layout
    refs = list(refs)
    where_ref = refs.pop(0)
    att_refs = [refs.pop(0) for _ in range(4)]
    x_ref, cot_ref, vec_ref, eb_ref = [refs.pop(0) for _ in range(4)]
    packed = [refs.pop(0) for _ in range(2 if aligned else 1)]
    out_ref, resid_ref = [refs.pop(0) for _ in range(2)]
    da_refs = [refs.pop(0) for _ in range(4)]
    vec_out = refs.pop(0)
    targets = [refs.pop(0) for _ in range(5 if aligned else 1)]
    wo, w1, w2, go, g1, g2, act, slope, in_sem, out_sem = refs
    group, zi, xi, ci, bi, start, length = [where_ref[i] for i in range(7)]
    rows, width = x_ref.shape

    def lanes(i):
        return slice(i * width, (i + 1) * width)

    weights = [wo, *[w1.at[k] for k in range(fold)], *[w2.at[k] for k in range(fold)]]
    block = n_b * own_rows
    for i, weight in enumerate(weights):
        if not aligned:
            pltpu.make_async_copy(packed[0].at[:, lanes(i)], weight, in_sem.at[i]).start()
            continue
        for half in range(2):
            for m in range(2 * n_q):
                src = packed[half].at[m * block : (m + 1) * block, lanes(i)]
                at = pl.ds(pl.multiple_of((2 * m + (ci ^ half)) * block, 16), block)
                pltpu.make_async_copy(src, weight.at[at], in_sem.at[i]).start()
    loads = [pltpu.make_async_copy(w, w, in_sem.at[i]) for i, w in enumerate(weights)]

    def group_rows(r):
        other = (2 * (xi ^ (r // 2))) + (ci ^ (r % 2))
        return pl.ds(pl.multiple_of(other * OWN_WIDTH, HEAD_DIM), OWN_WIDTH)

    obias, gain1, shift1, sbias, gain2, shift2 = [vec_ref[i : i + 1, :] for i in range(2, 8)]
    loads[0].wait()
    branch = obias + jnp.zeros((rows, width), f32)
    for r in range(4):
        branch += jnp.dot(att_refs[r][...], wo[group_rows(r), :], preferred_element_type=f32)
    hidden, normal1, inverse1 = norm_forward(x_ref[...].astype(f32) + branch, gain1, shift1)
    hidden_low = hidden.astype(bf16)
    shrunk = sbias + hidden
    for k in range(fold):
        loads[1 + k].wait()
        expanded = jnp.dot(hidden_low, w1[k], preferred_element_type=f32) + eb_ref[k : k + 1, :]
        cdf = 0.5 * (1.0 + lax.erf(expanded * (2.0**-0.5)))
        pdf = jnp.exp(-0.5 * expanded * expanded) * ((2.0 * math.pi) ** -0.5)
        act[k] = (expanded * cdf).astype(bf16)
        slope[k] = cdf + expanded * pdf
        loads[1 + fold + k].wait()
        shrunk += jnp.dot(act[k], w2[k], preferred_element_type=f32)
    result, normal2, inverse2 = norm_forward(shrunk, gain2, shift2)
    out_ref[...] = result.astype(bf16)
    row = lax.broadcasted_iota(jnp.int32, (rows, width), 0)
    seed = jnp.where(start + row < length, cot_ref[...].astype(f32), 0.0)
    vec_out[4:5, :] = jnp.sum(seed * normal2, axis=0, keepdims=True)
    vec_out[5:6, :] = jnp.sum(seed, axis=0, keepdims=True)
    resid2 = norm_backward(seed, gain2, normal2, inverse2)
    shrunk_low = resid2.astype(bf16)
    vec_out[3:4, :] = jnp.sum(shrunk_low.astype(f32), axis=0, keepdims=True)
    hidden_grad = resid2
    for k in range(fold):
        active_grad = lax.dot_general(
            shrunk_low, w2[k], CONTRACT_LAST, preferred_element_type=f32
        )
        expanded_low = (active_grad * slope[k]).astype(bf16)
        vec_out[8 + k : 9 + k, :] = jnp.sum(expanded_low.astype(f32), axis=0, keepdims=True)
        hidden_grad += lax.dot_general(
            expanded_low, w1[k], CONTRACT_LAST, preferred_element_type=f32
        )
        g2[k] = lax.dot_general(
            act[k], shrunk_low, CONTRACT_FIRST, preferred_element_type=f32
        ).astype(bf16)
        g1[k] = lax.dot_general(
            hidden_low, expanded_low, CONTRACT_FIRST, preferred_element_type=f32
        ).astype(bf16)
    vec_out[1:2, :] = jnp.sum(hidden_grad * normal1, axis=0, keepdims=True)
    vec_out[2:3, :] = jnp.sum(hidden_grad, axis=0, keepdims=True)
    resid1 = norm_backward(hidden_grad, gain1, normal1, inverse1)
    resid_ref[...] = resid1
    branch_low = resid1.astype(bf16)
    vec_out[0:1, :] = jnp.sum(branch_low.astype(f32), axis=0, keepdims=True)
    vec_out[6:8, :] = jnp.zeros((2, width), f32)
    vec_out[8 + fold :, :] = jnp.zeros((vec_out.shape[0] - 8 - fold, width), f32)
    for r in range(4):
        da_refs[r][...] = lax.dot_general(
            branch_low, wo[group_rows(r), :], CONTRACT_LAST, preferred_element_type=f32
        ).astype(bf16)
        go[group_rows(r), :] = lax.dot_general(
            att_refs[r][...], branch_low, CONTRACT_FIRST, preferred_element_type=f32
        ).astype(bf16)
    units = [g2.at[k] for k in range(fold)] + [g1.at[k] for k in range(fold)] + [go]
    if aligned:
        *parts, whole = unit_parts(fold)
        for i, part in enumerate(parts):
            for dc in range(2):
                target, sem = targets[2 * i + dc], out_sem.at[2 * i + dc]
                for dx in range(2):
                    for jz in range(n_q):
                        m = ((zi ^ jz) * 2 + (xi ^ dx)) * 2 + (ci ^ dc)
                        at = pl.ds(pl.multiple_of(m * block, 16), block)
                        for place, unit in enumerate(part):
                            dst = target.at[dx, jz, :, lanes(place)]
                            pltpu.make_async_copy(units[unit].at[at], dst, sem).start()
        for place, unit in enumerate(whole):
            dst = targets[-1].at[:, lanes(place)]
            pltpu.make_async_copy(units[unit], dst, out_sem.at[len(targets) - 1]).start()
    else:
        for i, unit in enumerate(units):
            pltpu.make_async_copy(unit, targets[0].at[:, lanes(i)], out_sem.at[0]).start()
    for i, dst in enumerate(targets):
        pltpu.make_async_copy(dst, dst, out_sem.at[i]).wait()


def unit_parts(fold):
    count = 1 + 2 * fold
    edges = [0, count // 3, (count + 1) // 2, count]
    return [range(edges[i], edges[i + 1]) for i in range(3)]


def ffn_block(layout, where, att, x, cot, vectors, ebias, packed):
    n_q, n_b, own_rows, fold, aligned = layout
    rows, width = x.shape
    ff = fold * width
    operands = [where, *att, x, cot, vectors, ebias, *[in_hbm(v) for v in packed]]
    in_specs = [pl.BlockSpec(memory_space=pltpu.SMEM)] + vmem_specs(8)
    in_specs += [pl.BlockSpec(memory_space=pltpu.HBM)] * len(packed)
    out_shape = [
        jax.ShapeDtypeStruct((rows, width), bf16),
        jax.ShapeDtypeStruct((rows, width), f32),
        *[jax.ShapeDtypeStruct((rows, OWN_WIDTH), bf16)] * 4,
        jax.ShapeDtypeStruct((16, width), f32),
    ]
    if aligned:
        lead = (2, n_q, n_b * own_rows)
        sizes = [len(part) * width for part in unit_parts(fold)]
        targets = [pltpu.HBM((*lead, size), bf16) for size in sizes[:-1] for _ in range(2)]
        targets.append(pltpu.HBM((width, sizes[-1]), bf16))
    else:
        targets = [pltpu.HBM((width, width + 2 * ff), bf16)]
    weight_scratch = [
        pltpu.VMEM((width, width), bf16),
        pltpu.VMEM((fold, width, width), bf16),
        pltpu.VMEM((fold, width, width), bf16),
    ]
    return pl.pallas_call(
        partial(ffn_kernel, layout),
        out_shape=out_shape + targets,
        in_specs=in_specs,
        out_specs=vmem_specs(len(out_shape)) + [pl.BlockSpec(memory_space=pltpu.HBM)] * len(targets),
        scratch_shapes=weight_scratch
        + weight_scratch
        + [
            pltpu.VMEM((fold, rows, width), bf16),
            pltpu.VMEM((fold, rows, width), f32),
            pltpu.SemaphoreType.DMA((1 + 2 * fold,)),
            pltpu.SemaphoreType.DMA((6,)),
        ],
        compiler_params=pltpu.CompilerParams(vmem_limit_bytes=32 * MIB),
        cost_estimate=pl.CostEstimate(
            flops=int(2e10), transcendentals=2 * rows * ff, bytes_accessed=int(3e7)
        ),
        name="feed_forward",
    )(*operands)


def order_kernel(n_q, n_b, where_ref, blocks_ref, out_ref):
    group, zi, bi = [where_ref[i] for i in range(3)]
    rows = blocks_ref.shape[3]
    for m in range(4 * n_q):
        q, g = m // 4, m % 4
        far, r = lax.rem(q + n_q - zi, n_q), g ^ group
        both = [
            blocks_ref[lax.rem(b + n_b - bi, n_b), far, r].astype(f32) for b in range(n_b)
        ]
        at = slice(m * n_b * rows, (m + 1) * n_b * rows)
        out_ref[at, :] = jnp.concatenate(both, axis=0).astype(bf16)


def order_rows(n_q, n_b, where, blocks):
    rows, lanes = blocks.shape[3:]
    return pl.pallas_call(
        partial(order_kernel, n_q, n_b),
        out_shape=jax.ShapeDtypeStruct((4 * n_q * n_b * rows, lanes), bf16),
        in_specs=[pl.BlockSpec(memory_space=pltpu.SMEM)] + vmem_specs(1),
        out_specs=vmem_specs(1)[0],
        compiler_params=pltpu.CompilerParams(vmem_limit_bytes=12 * MIB),
        name="order_rows",
    )(where, blocks)


def from_shift(value, axis, count, step):
    return lax.ppermute(value, axis, [((i + step) % count, i) for i in range(count)])


def square_swap(value, r):
    if r == 0:
        return value
    if r == 1:
        return lax.ppermute(value, "c", [(0, 1), (1, 0)])
    if r == 2:
        return lax.ppermute(value, "x", [(0, 1), (1, 0)])
    return lax.ppermute(value, ("x", "c"), [(0, 3), (3, 0), (1, 2), (2, 1)])


def pick(stacked, index, dim=0):
    return lax.dynamic_index_in_dim(stacked, index, dim, keepdims=False)


class Chain:
    def __init__(self, state, *steps):
        self.state, self.steps = tuple(state), list(steps)


def launch(chain):
    chain.state = tuple(chain.steps.pop(0)(*chain.state))


def run_stage(chains, outs=(), settle=()):
    for chain in chains:
        launch(chain)
    joined = [*chains, *settle]
    outs, states = lax.optimization_barrier((tuple(outs), [c.state for c in joined]))
    for chain, state in zip(joined, states):
        chain.state = tuple(state)
    return outs


def away_sum(total, axis, count):
    parts = [total[j].astype(bf16) for j in range(1, count)]
    return [from_shift(part, axis, count, count - j - 1) for j, part in enumerate(parts)]


def weight_sum(keep, send, n_q, n_b, bi, order):
    def own_b(keep, got, j):
        shape = (2, n_q, n_b, -1, keep.shape[-1])
        both = [pick(v.reshape(shape), (bi + j) % n_b, 2).astype(f32) for v in (keep, got)]
        return both[0] + both[1]

    def over_core(keep, send):
        return keep, square_swap(send, 1)

    def over_b(keep, got):
        if order:
            keep = lax.optimization_barrier((keep, order.pop()))[0]
        away = [own_b(keep, got, j).astype(bf16) for j in range(1, n_b)]
        order.append(away[0])
        return keep, got, *[from_shift(v, "b", n_b, n_b - 1 - j) for j, v in enumerate(away)]

    def over_x(keep, got, *more):
        total = own_b(keep, got, 0) + sum(v.astype(f32) for v in more)
        return total[0], *away_sum(total, "x", 2)

    def halve(half):
        def over_q(own, got):
            total = own + got.astype(f32)
            pairs = [(i, i ^ half) for i in range(n_q)]
            return total[:half], lax.ppermute(total[half:].astype(bf16), "q", pairs)

        return over_q

    halves = [n_q >> (k + 1) for k in range(n_q.bit_length() - 1)]
    return Chain((keep, send), over_core, over_b, over_x, *[halve(half) for half in halves])


def toward(j, n_q):
    return (j - 1, n_q - 1) if 2 * j <= n_q else ((j + 1) % n_q, 1)


def token_sum(keep, send, n_q, j, farther):
    def over_core(keep, send):
        return keep, square_swap(send, 1)

    def over_x(keep, got):
        total = keep.astype(f32) + got.astype(f32)
        return total[0], square_swap(total[1].astype(bf16), 2)

    def over_q(own, got):
        total = own + got.astype(f32) + sum(chain_sum(c) for c in farther)
        return (from_shift(total.astype(bf16), "q", n_q, toward(j, n_q)[1]),)

    return Chain((keep, send), over_core, over_x, *([over_q] if j else []))


def chain_sum(chain):
    return sum(v.astype(f32).reshape(chain.state[0].shape) for v in chain.state)


def deinterleave(fold):
    size = fold * LANES
    lane = jnp.arange(size)
    return (lane[:, None] // fold + (lane[:, None] % fold) * LANES == lane[None, :]).astype(bf16)


def per_device(
    n_q,
    n_b,
    inputs,
    lengths,
    cotangent,
    triple_weight,
    query_bias,
    value_bias,
    output_weight,
    output_bias,
    first_gain,
    first_shift,
    expand_weight,
    expand_bias,
    shrink_weight,
    shrink_bias,
    second_gain,
    second_shift,
):
    zi, xi, ci, bi = [lax.axis_index(a) for a in AXES]
    group = 2 * xi + ci
    _, seq_rows, width = inputs.shape
    own_rows = triple_weight.shape[0]
    ff = expand_weight.shape[1]
    fold = ff // width
    aligned = n_b * own_rows % 16 == 0 and n_q & (n_q - 1) == 0
    x_own = inputs[0]

    turn = deinterleave(fold)
    expand_own = expand_weight.astype(bf16).reshape(own_rows, -1, fold * LANES)
    expand_own = jnp.einsum("rbs,st->rbt", expand_own, turn, preferred_element_type=f32)
    expand_own = expand_own.astype(bf16).reshape(own_rows, -1, fold, LANES).transpose(0, 2, 1, 3)
    packed = jnp.concatenate(
        [
            output_weight.astype(bf16),
            expand_own.reshape(own_rows, ff),
            shrink_weight.astype(bf16).reshape(own_rows, ff),
        ],
        axis=1,
    )
    if aligned:
        own_half = lax.all_gather(packed, ("q", "x", "b"), axis=0, tiled=True)
    else:
        gathered_ffn = [lax.all_gather(packed, AXES, axis=0, tiled=True)]

    names = [query_bias, value_bias, output_bias, first_gain, first_shift]
    names += [shrink_bias, second_gain, second_shift]
    vectors = jnp.stack(names, axis=1)
    vectors = jnp.concatenate([vectors, expand_bias.reshape(own_rows, fold)], axis=1).astype(bf16)
    n_vec = vectors.shape[1]
    vectors = jnp.pad(vectors, ((0, 0), (0, WIDE - VECTORS - n_vec)))
    thirds = triple_weight.astype(bf16).reshape(own_rows, 3, GROUPS, OWN_WIDTH)

    def columns_of(g):
        mine = [pick(thirds[:, t], g, 1) for t in range(3)]
        return jnp.concatenate(mine + [vectors], axis=1)

    def rows_square(*blocks):
        return [square_swap(block, r) for r, block in enumerate(blocks)]

    def rows_q(*blocks):
        square = jnp.stack(blocks)
        return [square] + [from_shift(square, "q", n_q, j) for j in range(1, n_q)]

    def rows_b(*blocks):
        both = jnp.stack(blocks)
        return [both] + [from_shift(both, "b", n_b, j) for j in range(1, n_b)]

    weight_rows = Chain([columns_of(group ^ r) for r in range(4)], rows_square, rows_q, rows_b)

    def token_chunk(j):
        def over_q():
            source, step = toward(j, n_q)
            own = chunks[source].state[0] if source else x_own
            if j not in arrival[:2]:
                at = arrival.index(j)
                before = line[at - 1].state[0] if at > 2 else weight_rows.state
                own = lax.optimization_barrier((own, before))[0]
            return (from_shift(own, "q", n_q, n_q - step),)

        def over_x(own):
            return own, square_swap(own, 2)

        def over_core(own, other):
            halves = square_swap(jnp.stack([own, other]), 1)
            return own, halves[0], other, halves[1]

        return Chain(() if j else (x_own,), *([over_q] if j else []), over_x, over_core)

    arrival = []
    for j in [k for pair in zip(range(1, n_q), range(n_q - 1, 0, -1)) for k in pair]:
        arrival += [] if j in arrival else [j]
    arrival = [0] + arrival
    chunks = {j: token_chunk(j) for j in arrival}
    line = [chunks[j] for j in arrival]


    for slot in range(3):
        ready = line[:2] if slot < 2 else line[1:3]
        run_stage([c for c in ready if c.steps] + [weight_rows])
    chunk_x = {}

    by_distance = jnp.stack(weight_rows.state)
    if aligned:
        spot = jnp.stack([group, zi, bi]).astype(jnp.int32)
        w_own = order_rows(n_q, n_b, spot, by_distance)
    else:
        ordered = jnp.stack([pick(by_distance, (i - bi) % n_b) for i in range(n_b)], axis=3)
        ordered = jnp.stack([pick(ordered, group ^ g, 1) for g in range(4)], axis=1)
        ordered = jnp.stack([pick(ordered, (i - zi) % n_q) for i in range(n_q)])
        w_own = ordered.transpose(0, 1, 3, 2, 4).reshape(width, WIDE)
    turned = w_own[:, VECTORS : VECTORS + n_vec].astype(f32)
    turned = turned.T
    ebias = turned[8:]
    turned = turned[:8]
    own_bias = lax.dynamic_slice_in_dim(turned, group * OWN_WIDTH, OWN_WIDTH, 1)
    zero = jnp.zeros((1, OWN_WIDTH), f32)
    bias_row = jnp.concatenate(
        [own_bias[:1], zero, own_bias[1:2], jnp.zeros((1, WIDE - VECTORS), f32)], axis=1
    )

    def where_of(j):
        zj = (zi + j) % n_q
        spots = [(zj * 4 + (group ^ r)) * seq_rows for r in range(4)]
        return jnp.stack(spots + [lengths[0]]).astype(jnp.int32)

    weights = (w_own, bias_row)
    kept = {}
    carry = None
    for step, j in enumerate(arrival):
        first, last = step == 0, step == n_q - 1
        if chunks[j].steps:
            run_stage([chunks[j]])
        chunk_x[j] = chunks[j].state
        outs = attend_chunk(first, last, where_of(j), chunk_x[j], weights, carry)
        ready = line[max(2, step + 1) : step + 4]
        outs = run_stage([c for c in ready if c.steps], outs)
        kept[j] = (outs[0], outs[1])
        outs = outs[2:]
        if first:
            qx, qp = outs[:2]
            outs = outs[2:]
        carry = (qx, *outs)
    att, attx, qx2 = carry[1:5], carry[5], carry[6]

    if aligned:
        own_half, att = lax.optimization_barrier((own_half, att))
        gathered_ffn = [own_half, square_swap(own_half, 1)]
    att = [square_swap(att[r], r) for r in range(4)]
    start = (zi * 4 + group) * seq_rows
    where = jnp.stack([group, zi, xi, ci, bi, start, lengths[0]]).astype(jnp.int32)
    layout = (n_q, n_b, own_rows, fold, aligned)
    outs = ffn_block(layout, where, att, x_own, cotangent[0], turned, ebias, gathered_ffn)
    output, resid_first_grad = outs[:2]
    att_grads, vec_grads, summands = outs[2:6], outs[6], outs[7:]
    square = Chain(att_grads, lambda *parts: [square_swap(v, r) for r, v in enumerate(parts)])

    sums, order = [], []
    if aligned:
        for i in range(2):
            sums.append(weight_sum(summands[2 * i], summands[2 * i + 1], n_q, n_b, bi, order))
    reduced = lax.psum_scatter(summands[-1], AXES, scatter_dimension=0, tiled=True)
    run_stage([square] + sums)
    plan = [([0], [], [1]), ([0], [1], []), ([1, 0], [], []), ([1, 0], [], [])]
    shared = (qx2, qp, w_own, square.state, attx)
    carry = None
    moving, moving_to = [], {}
    for step, j in enumerate(reversed(arrival)):
        first, last = step == 0, step == n_q - 1
        with_it, ending, going_on = [], [], []
        if sums and step < len(plan):
            with_it, ending, going_on = [[sums[i] for i in part] for part in plan[step]]
        outs = attend_back_chunk(first, last, kept[j], chunk_x[j], shared, carry)
        run = with_it + [c for c in moving if c.steps]
        for chain in run + going_on:
            launch(chain)
        free = outs[2:] if last else []
        outs = run_stage([], outs[:2] if last else outs, settle=run + ending)
        outs = (*outs, *free)
        keep, send = outs[:2]
        farther = [c for k, c in moving_to.items() if k and toward(k, n_q)[0] == j and j]
        moving_to[j] = token_sum(keep, send, n_q, j, farther)
        moving.append(moving_to[j])
        outs = outs[2:]
        if first:
            dox = outs[0]
            outs = outs[1:]
        carry = (dox, *outs)
        if not last:
            carry = run_stage(moving[-1:], carry)
    grad_joint, col = carry[1:]

    own_bias = jnp.stack([col[0, :OWN_WIDTH], col[0, 2 * OWN_WIDTH : 3 * OWN_WIDTH]])
    bias_grads = lax.dynamic_update_slice(
        jnp.zeros((2, width), f32), own_bias, (0, group * OWN_WIDTH)
    )
    tall = jnp.concatenate([bias_grads, vec_grads[:6], vec_grads[8 : 8 + fold]], axis=0).T
    tall_high = tall.astype(bf16)
    tall_low = (tall - tall_high.astype(f32)).astype(bf16)
    room = jnp.zeros((width, WIDE - VECTORS - 2 * n_vec), bf16)
    blocks = jnp.concatenate([grad_joint[:, :VECTORS], tall_high, tall_low, room], axis=1)
    total = blocks.reshape(n_q, 4, n_b, own_rows, WIDE)

    def rows_over_b(total):
        parts = [pick(total, (bi + j) % n_b, 2) for j in range(n_b)]
        return parts[0], *away_sum(parts, "b", n_b)

    def rows_over_q(*parts):
        total = sum(v.astype(f32) for v in parts)
        parts = [pick(total, (zi + j) % n_q) for j in range(n_q)]
        return parts[0], *away_sum(parts, "q", n_q)

    def rows_over_square(*parts):
        total = sum(v.astype(f32) for v in parts).astype(bf16)
        return [square_swap(pick(total, group ^ r), r) for r in range(4)]

    rows = Chain((total,), rows_over_b, rows_over_q, rows_over_square)
    while any(c.steps for c in [rows, *sums, *moving]):
        run_stage([c for c in [rows, *sums, *moving] if c.steps])
        if len(rows.steps) == 1:
            reduced, rows.state = lax.optimization_barrier((reduced, rows.state))
    summed = reduced.astype(f32)
    token_grad = resid_first_grad
    for j, chain in moving_to.items():
        if j == 0 or toward(j, n_q)[0] == 0:
            token_grad = token_grad + chain_sum(chain)
    input_grad = token_grad.astype(bf16)
    if aligned:
        summed = jnp.concatenate([*[chain_sum(c)[0] for c in sums], summed], axis=1)
    parts = jnp.stack(rows.state)
    parts = jnp.stack([pick(parts, group ^ g) for g in range(4)])
    grad_triple = parts[:, :, :VECTORS].reshape(GROUPS, own_rows, 3, OWN_WIDTH)
    grad_triple = grad_triple.transpose(1, 2, 0, 3).reshape(own_rows, -1).astype(f32)
    small = jnp.sum(parts[:, :, VECTORS : VECTORS + 2 * n_vec].astype(f32), axis=0)
    small = small[:, :n_vec] + small[:, n_vec:]
    grad_expand = summed[:, ff : 2 * ff].reshape(own_rows, fold, -1, LANES).transpose(0, 2, 1, 3)
    grad_expand = jnp.einsum(
        "rbs,ts->rbt",
        grad_expand.reshape(own_rows, -1, fold * LANES),
        turn.astype(f32),
        precision=lax.Precision.HIGHEST,
        preferred_element_type=f32,
    ).reshape(own_rows, ff)
    return (
        output[None],
        input_grad[None],
        grad_triple,
        small[:, 0],
        small[:, 1],
        summed[:, 2 * ff :],
        small[:, 2],
        small[:, 3],
        small[:, 4],
        grad_expand,
        small[:, 8:].reshape(-1),
        summed[:, :ff].reshape(-1, width),
        small[:, 5],
        small[:, 6],
        small[:, 7],
    )


def solution(mesh):
    n_seq, n_b = mesh.shape["seq"], mesh.shape["batch"]
    n_q = n_seq // GROUPS
    fine = Mesh(mesh.devices.reshape(n_q, 2, 2, n_b), AXES)
    tokens = P("b", ("q", "x", "c"), None)
    matrix = P(AXES, None)
    vector = P(AXES)
    in_specs = (
        tokens,
        P("b"),
        tokens,
        matrix,
        vector,
        vector,
        matrix,
        vector,
        vector,
        vector,
        matrix,
        vector,
        matrix,
        vector,
        vector,
        vector,
    )
    out_specs = (
        tokens,
        tokens,
        matrix,
        vector,
        vector,
        matrix,
        vector,
        vector,
        vector,
        matrix,
        vector,
        matrix,
        vector,
        vector,
        vector,
    )
    return jax.shard_map(
        partial(per_device, n_q, n_b),
        mesh=fine,
        in_specs=in_specs,
        out_specs=out_specs,
        check_vma=False,
    )
```

profile of v0, /device:TPU:0, one launch (start us, length us, event | category | flops | bytes accessed | tf_op | source)
XLA Modules:
  0.0 331.0 jit_solution(13011623397469160465)
XLA Ops:
  10.1 3.0 collective-permute-start
  13.1 3.6 %collective-permute-start.1 = (bf16[256,768]{1,0:T(8,128)(2,1)S(1)}, bf16[256,768]{1,0:T(8,128)(2,1)}, u32[]{:S(2)}, u32[]{:S(2)}) collective-permute-start(bf16[256,768]{1,0:T(8,128)(2,1)S(1)} %bitcast.226), channel_id=1, source_target_pairs={{8,0},{16,8},{24,16},{0,24},{9,1},{17,9},{25,17},{1,25},{10,2},{18... | collective-permute-start | bytes 1179656 | tf_op jit(solution)/shard_map/ppermute | solution.py:582
  20.7 2.4 collective-permute-done.3
  23.3 4.0 %collective-permute-done.1.refs_1_.refs_3_ = bf16[256,768]{1,0:T(8,128)(2,1)} collective-permute-done((bf16[256,768]{1,0:T(8,128)(2,1)S(1)}, bf16[256,768]{1,0:T(8,128)(2,1)}, u32[]{:S(2)}, u32[]{:S(2)}) %collective-permute-start.1) | collective-permute-done | bytes 393248 | tf_op jit(solution)/shard_map/ppermute | solution.py:582
  27.6 4.4 %collective-permute-start.7 = (bf16[4,24,640]{2,1,0:T(8,128)(2,1)S(1)}, bf16[4,24,640]{2,1,0:T(8,128)(2,1)S(1)}, u32[]{:S(2)}, u32[]{:S(2)}) collective-permute-start(bf16[4,24,640]{2,1,0:T(8,128)(2,1)S(1)} %pad_maximum_fusion.9), channel_id=1, source_target_pairs={{8,0},{16,8},{24,16},{0,24},{9,1},{17,9},{25,17},{1,25},{10,2},{18... | collective-permute-start | bytes 368648 | tf_op jit(solution)/shard_map/ppermute | solution.py:582
  33.6 5.4 %collective-permute-done.7 = bf16[4,24,640]{2,1,0:T(8,128)(2,1)S(1)} collective-permute-done((bf16[4,24,640]{2,1,0:T(8,128)(2,1)S(1)}, bf16[4,24,640]{2,1,0:T(8,128)(2,1)S(1)}, u32[]{:S(2)}, u32[]{:S(2)}) %collective-permute-start.7) | collective-permute-done | bytes 122912 | tf_op jit(solution)/shard_map/ppermute | solution.py:582
  39.0 5.6 %collective-permute-done.8 = bf16[4,24,640]{2,1,0:T(8,128)(2,1)S(1)} collective-permute-done((bf16[4,24,640]{2,1,0:T(8,128)(2,1)S(1)}, bf16[4,24,640]{2,1,0:T(8,128)(2,1)S(1)}, u32[]{:S(2)}, u32[]{:S(2)}) %collective-permute-start.8) | collective-permute-done | bytes 122912 | tf_op jit(solution)/shard_map/ppermute | solution.py:582
  50.1 19.3 %collective-permute-done.11.refs_1_.refs_3_ = bf16[256,768]{1,0:T(8,128)(2,1)} collective-permute-done((bf16[256,768]{1,0:T(8,128)(2,1)S(1)}, bf16[256,768]{1,0:T(8,128)(2,1)}, u32[]{:S(2)}, u32[]{:S(2)}) %collective-permute-start.11) | collective-permute-done | bytes 393248 | tf_op jit(solution)/shard_map/ppermute | solution.py:582
  70.5 5.8 %collective-permute-start.14 = (bf16[256,768]{1,0:T(8,128)(2,1)}, bf16[256,768]{1,0:T(8,128)(2,1)}, u32[]{:S(2)}, u32[]{:S(2)}) collective-permute-start(bf16[256,768]{1,0:T(8,128)(2,1)} %collective-permute-done.1.refs_1_.refs_3_), channel_id=1, source_target_pairs={{8,0},{16,8},{24,16},{0,24},{9,1},{17,9},{25,17},{1,25},{10,2},{18... | collective-permute-start | bytes 1179656 | tf_op jit(solution)/shard_map/ppermute | solution.py:582
  78.1 8.6 %attend_forward.4 = (bf16[3,1024,256]{2,1,0:T(8,128)(2,1)}, bf16[3,1024,128]{2,1,0:T(8,128)(2,1)}, bf16[3,1024,256]{2,1,0:T(8,128)(2,1)S(1)}, bf16[3,1024,128]{2...) custom-call(s32[5]{0:T(128)S(1)} %stack.273.refs_0_, bf16[256,768]{1,0:T(8,128)(2,1)} %bitcast.223, ...), custom_call_target="tpu_custom_call" | custom-call | flops 8000000000 | bytes 10000000 | tf_op jit(solution)/shard_map/attend_forward/pallas_call | solution.py:190
  88.6 4.7 %collective-permute-done.14.refs_1_.refs_3_ = bf16[256,768]{1,0:T(8,128)(2,1)} collective-permute-done((bf16[256,768]{1,0:T(8,128)(2,1)}, bf16[256,768]{1,0:T(8,128)(2,1)}, u32[]{:S(2)}, u32[]{:S(2)}) %collective-permute-start.14) | collective-permute-done | bytes 393248 | tf_op jit(solution)/shard_map/ppermute | solution.py:582
  93.4 2.1 pad_maximum_fusion.3
  96.8 9.2 %attend_forward.5 = (bf16[3,1024,256]{2,1,0:T(8,128)(2,1)}, bf16[3,1024,128]{2,1,0:T(8,128)(2,1)}, f32[3,8,1024]{2,1,0:T(8,128)S(1)}, f32[3,80,1024]{2,1,0:T(8,128)S(1)}) custom-call(s32[5]{0:T(128)S(1)} %stack.240.refs_0_, bf16[256,768]{1,0:T(8,128)(2,1)} %collective-permute-done.1.refs_1_.refs_3_, bf16[256,768]{1,0:T(8,128)(2,1)} %get-tuple-element.233.refs_2_.refs_4_, ...), custom_call_target="tpu_custom_call" | custom-call | flops 8000000000 | bytes 10000000 | tf_op jit(solution)/shard_map/attend_forward/pallas_call | solution.py:190
  110.9 9.2 %attend_forward.6 = (bf16[3,1024,256]{2,1,0:T(8,128)(2,1)}, bf16[3,1024,128]{2,1,0:T(8,128)(2,1)}, f32[3,8,1024]{2,1,0:T(8,128)S(1)}, f32[3,80,1024]{2,1,0:T(8,128)S(1)}) custom-call(s32[5]{0:T(128)S(1)} %stack.235.refs_0_, bf16[256,768]{1,0:T(8,128)(2,1)} %collective-permute-done.11.refs_1_.refs_3_, bf16[256,768]{1,0:T(8,128)(2,1)} %get-tuple-element.261.refs_2_.refs_4_, ...), custom_call_target="tpu_custom_call" | custom-call | flops 8000000000 | bytes 10000000 | tf_op jit(solution)/shard_map/attend_forward/pallas_call | solution.py:190
  120.1 2.2 slice_bitcast_fusion.6
  122.3 9.1 %attend_forward.7 = (bf16[3,1024,256]{2,1,0:T(8,128)(2,1)}, bf16[3,1024,128]{2,1,0:T(8,128)(2,1)}, bf16[256,192]{1,0:T(8,128)(2,1)S(1)}, bf16[256,192]{1,0:T(8,1...) custom-call(s32[5]{0:T(128)S(1)} %stack.230.refs_0_, ...), custom_call_target="tpu_custom_call" | custom-call | flops 8000000000 | bytes 10000000 | tf_op jit(solution)/shard_map/attend_forward/pallas_call | solution.py:190
  136.3 3.9 %collective-permute-done.18.refs_2_ = bf16[256,192]{1,0:T(8,128)(2,1)S(1)} collective-permute-done((bf16[256,192]{1,0:T(8,128)(2,1)S(1)}, bf16[256,192]{1,0:T(8,128)(2,1)S(1)}, u32[]{:S(2)}, u32[]{:S(2)}) %collective-permute-start.18) | collective-permute-done | bytes 98336 | tf_op jit(solution)/shard_map/ppermute | solution.py:589
  143.2 18.8 %feed_forward.1 = (bf16[256,768]{1,0:T(8,128)(2,1)}, f32[256,768]{1,0:T(8,128)S(1)}, bf16[256,192]{1,0:T(8,128)(2,1)S(1)}, bf16[256,192]{1,0:T(8,128)(2,1)S(1)},...) custom-call(s32[7]{0:T(128)S(1)} %stack.225.refs_0_, ...), custom_call_target="tpu_custom_call" | custom-call | flops 20000000000 | bytes 30000000 | tf_op jit(solution)/shard_map/feed_forward/pallas_call | solution.py:535
  166.1 2.9 collective-permute-done.23.refs_11_
  176.4 11.9 %attend_backward.4 = (bf16[2,256,768]{2,1,0:T(8,128)(2,1)S(1)}, bf16[2,256,768]{2,1,0:T(8,128)(2,1)S(1)}, bf16[3,1024,128]{2,1,0:T(8,128)(2,1)S(1)}, f32[3,64,10...) custom-call(bf16[3,1024,256]{2,1,0:T(8,128)(2,1)} %get-tuple-element.293.refs_0_, ...), custom_call_target="tpu_custom_call" | custom-call | flops 15000000512 | bytes 10000000 | tf_op jit(solution)/shard_map/attend_backward/pallas_call | solution.py:356
  188.4 7.0 %collective-permute-done.27 = bf16[2,4,24,2304]{3,2,1,0:T(8,128)(2,1)S(1)} collective-permute-done((bf16[2,4,24,2304]{3,2,1,0:T(8,128)(2,1)S(1)}, bf16[2,4,24,2304]{3,2,1,0:T(8,128)(2,1)S(1)}, u32[]{:S(2)}, u32[]{:S(2)}) %collective-permute-start.27) | collective-permute-done | bytes 884768 | tf_op jit(solution)/shard_map/ppermute | solution.py:582
  199.4 11.6 %attend_backward.5 = (bf16[2,256,768]{2,1,0:T(8,128)(2,1)S(1)}, bf16[2,256,768]{2,1,0:T(8,128)(2,1)S(1)}, f32[3,64,1024]{2,1,0:T(8,128)S(1)}, f32[768,512]{1,0:T(8,128)S(1)}, f32[8,512]{1,0:T(8,128)S(1)}) custom-call(bf16[3,1024,256]{2,1,0:T(8,128)(2,1)} %get-tuple-element.319.refs_0_, bf16[3,1024,128]{2,1,0:T(8,128)(2,1)} %get-tuple-element.320.refs_1_, ...), custom_call_target="tpu_custom_call" | custom-call | flops 15000000512 | bytes 10000000 | tf_op jit(solution)/shard_map/attend_backward/pallas_call | solution.py:356
  211.2 6.8 %collective-permute-done.30 = bf16[256,768]{1,0:T(8,128)(2,1)S(1)} collective-permute-done((bf16[256,768]{1,0:T(8,128)(2,1)S(1)}, bf16[256,768]{1,0:T(8,128)(2,1)S(1)}, u32[]{:S(2)}, u32[]{:S(2)}) %collective-permute-start.30) | collective-permute-done | bytes 393248 | tf_op jit(solution)/shard_map/ppermute | solution.py:591
  218.6 4.8 %collective-permute-start.34 = (bf16[2,24,2304]{2,1,0:T(8,128)(2,1)S(1)}, bf16[2,24,2304]{2,1,0:T(8,128)(2,1)S(1)}, u32[]{:S(2)}, u32[]{:S(2)}) collective-permute-start(bf16[2,24,2304]{2,1,0:T(8,128)(2,1)S(1)} %slice.343), channel_id=1, source_target_pairs={{0,16},{8,24},{16,0},{24,8},{1,17},{9,25},{17,1},{25,9},{2,18},{10... | collective-permute-start | bytes 663560 | tf_op jit(solution)/shard_map/ppermute | solution.py:647
  227.2 11.4 %attend_backward.6 = (bf16[2,256,768]{2,1,0:T(8,128)(2,1)S(1)}, bf16[2,256,768]{2,1,0:T(8,128)(2,1)S(1)}, f32[3,64,1024]{2,1,0:T(8,128)S(1)}, f32[768,512]{1,0:T(8,128)S(1)}, f32[8,512]{1,0:T(8,128)S(1)}) custom-call(bf16[3,1024,256]{2,1,0:T(8,128)(2,1)} %get-tuple-element.317.refs_0_, bf16[3,1024,128]{2,1,0:T(8,128)(2,1)} %get-tuple-element.318.refs_1_, ...), custom_call_target="tpu_custom_call" | custom-call | flops 15000000512 | bytes 10000000 | tf_op jit(solution)/shard_map/attend_backward/pallas_call | solution.py:356
  238.7 12.7 %collective-permute-done.34 = bf16[2,24,2304]{2,1,0:T(8,128)(2,1)S(1)} collective-permute-done((bf16[2,24,2304]{2,1,0:T(8,128)(2,1)S(1)}, bf16[2,24,2304]{2,1,0:T(8,128)(2,1)S(1)}, u32[]{:S(2)}, u32[]{:S(2)}) %collective-permute-start.34) | collective-permute-done | bytes 221216 | tf_op jit(solution)/shard_map/ppermute | solution.py:647
  258.6 12.2 %attend_backward.7 = (bf16[2,256,768]{2,1,0:T(8,128)(2,1)S(1)}, bf16[2,256,768]{2,1,0:T(8,128)(2,1)S(1)}, bf16[768,640]{1,0:T(8,128)(2,1)S(1)}, f32[8,640]{1,0:T(8,128)S(1)}) custom-call(bf16[3,1024,256]{2,1,0:T(8,128)(2,1)} %get-tuple-element.289.refs_0_, bf16[3,1024,128]{2,1,0:T(8,128)(2,1)} %get-tuple-element.290.refs_1_, bf16[768,640]{1,0:T(8,128)(2,1)} %copy-done, ...), custom_call_target="tpu_custom_call" | custom-call | flops 15000000512 | bytes 10000000 | tf_op jit(solution)/shard_map/attend_backward/pallas_call | solution.py:356
  282.3 2.1 collective-permute-start.43
  285.4 10.7 %collective-permute-done.43 = bf16[1,24,1536]{2,1,0:T(8,128)(2,1)S(1)} collective-permute-done((bf16[1,24,1536]{2,1,0:T(8,128)(2,1)S(1)}, bf16[1,24,1536]{2,1,0:T(8,128)(2,1)S(1)}, u32[]{:S(2)}, u32[]{:S(2)}) %collective-permute-start.43) | collective-permute-done | bytes 73760 | tf_op jit(solution)/shard_map/ppermute | solution.py:647
  298.4 2.3 collective-permute-start.47
  302.3 4.1 %collective-permute-done.46 = bf16[4,24,640]{2,1,0:T(8,128)(2,1)S(1)} collective-permute-done((bf16[4,24,640]{2,1,0:T(8,128)(2,1)S(1)}, bf16[4,24,640]{2,1,0:T(8,128)(2,1)S(1)}, u32[]{:S(2)}, u32[]{:S(2)}) %collective-permute-start.46) | collective-permute-done | bytes 122912 | tf_op jit(solution)/shard_map/ppermute | solution.py:582
  306.5 4.2 %collective-permute-done.47 = bf16[4,24,640]{2,1,0:T(8,128)(2,1)S(1)} collective-permute-done((bf16[4,24,640]{2,1,0:T(8,128)(2,1)S(1)}, bf16[4,24,640]{2,1,0:T(8,128)(2,1)S(1)}, u32[]{:S(2)}, u32[]{:S(2)}) %collective-permute-start.47) | collective-permute-done | bytes 122912 | tf_op jit(solution)/shard_map/ppermute | solution.py:582
  (330 shorter events, 87.6 us)
Async XLA Ops:
  7.2 126.7 %all-gather.2.cloned.1.call-start = ((), (), s32[]{:S(2)}) async-start(), calls=%async_computation.1 | async-start | bytes 5640192 | tf_op jit(solution)/shard_map/all_gather | solution.py:726
  10.0 300.6 %reduce-scatter.2.cloned.1.call-start = ((), (), s32[]{:S(2)}) async-start(), calls=%async_computation.2 | async-start | bytes 4866048 | tf_op jit(solution)/shard_map/reduce_scatter | solution.py:846
  10.1 13.2 %collective-permute-start = (bf16[256,768]{1,0:T(8,128)(2,1)S(1)}, bf16[256,768]{1,0:T(8,128)(2,1)S(1)}, u32[]{:S(2)}, u32[]{:S(2)}) collective-permute-start(bf16[256,768]{1,0:T(8,128)(2,1)S(1)} %bitcast.225), channel_id=1, source_target_pairs={{0,4},{4,0},{1,5},{5,1},{2,6},{6,2},{3,7},{7,3},{8,12},{12,8},{9,1... | collective-permute-start | bytes 1179656 | tf_op jit(solution)/shard_map/ppermute | solution.py:591
  13.1 14.2 %collective-permute-start.1 = (bf16[256,768]{1,0:T(8,128)(2,1)S(1)}, bf16[256,768]{1,0:T(8,128)(2,1)}, u32[]{:S(2)}, u32[]{:S(2)}) collective-permute-start(bf16[256,768]{1,0:T(8,128)(2,1)S(1)} %bitcast.226), channel_id=1, source_target_pairs={{8,0},{16,8},{24,16},{0,24},{9,1},{17,9},{25,17},{1,25},{10,2},{18... | collective-permute-start | bytes 1179656 | tf_op jit(solution)/shard_map/ppermute | solution.py:582
  27.5 17.2 %collective-permute-start.6 = (bf16[256,768]{1,0:T(8,128)(2,1)}, bf16[256,768]{1,0:T(8,128)(2,1)S(1)}, u32[]{:S(2)}, u32[]{:S(2)}) collective-permute-start(bf16[256,768]{1,0:T(8,128)(2,1)} %collective-permute-done.1.refs_1_.refs_3_), channel_id=1, source_target_pairs={{0,4},{4,0},{1,5},{5,1},{2,6},{6,2},{3,7},{7,3},{8,12},{12,8},{9,1... | collective-permute-start | bytes 1179656 | tf_op jit(solution)/shard_map/ppermute | solution.py:591
  27.6 11.4 %collective-permute-start.7 = (bf16[4,24,640]{2,1,0:T(8,128)(2,1)S(1)}, bf16[4,24,640]{2,1,0:T(8,128)(2,1)S(1)}, u32[]{:S(2)}, u32[]{:S(2)}) collective-permute-start(bf16[4,24,640]{2,1,0:T(8,128)(2,1)S(1)} %pad_maximum_fusion.9), channel_id=1, source_target_pairs={{8,0},{16,8},{24,16},{0,24},{9,1},{17,9},{25,17},{1,25},{10,2},{18... | collective-permute-start | bytes 368648 | tf_op jit(solution)/shard_map/ppermute | solution.py:582
  32.0 12.6 %collective-permute-start.8 = (bf16[4,24,640]{2,1,0:T(8,128)(2,1)S(1)}, bf16[4,24,640]{2,1,0:T(8,128)(2,1)S(1)}, u32[]{:S(2)}, u32[]{:S(2)}) collective-permute-start(bf16[4,24,640]{2,1,0:T(8,128)(2,1)S(1)} %pad_maximum_fusion.9), channel_id=1, source_target_pairs={{16,0},{24,8},{0,16},{8,24},{17,1},{25,9},{1,17},{9,25},{18,2},{26... | collective-permute-start | bytes 368648 | tf_op jit(solution)/shard_map/ppermute | solution.py:582
  32.0 12.6 %collective-permute-start.9 = (bf16[4,24,640]{2,1,0:T(8,128)(2,1)S(1)}, bf16[4,24,640]{2,1,0:T(8,128)(2,1)S(1)}, u32[]{:S(2)}, u32[]{:S(2)}) collective-permute-start(bf16[4,24,640]{2,1,0:T(8,128)(2,1)S(1)} %pad_maximum_fusion.9), channel_id=1, source_target_pairs={{24,0},{0,8},{8,16},{16,24},{25,1},{1,9},{9,17},{17,25},{26,2},{2,... | collective-permute-start | bytes 368648 | tf_op jit(solution)/shard_map/ppermute | solution.py:582
  46.0 23.4 %collective-permute-start.12 = (bf16[4,4,24,640]{3,2,1,0:T(8,128)(2,1)S(1)}, bf16[4,4,24,640]{3,2,1,0:T(8,128)(2,1)S(1)}, u32[]{:S(2)}, u32[]{:S(2)}) collective-permute-start(bf16[4,4,24,640]{3,2,1,0:T(8,128)(2,1)S(1)} %pad_maximum_fusion.5), channel_id=1, source_target_pairs={{1,0},{0,1},{3,2},{2,3},{5,4},{4,5},{7,6},{6,7},{9,8},{8,9},{11,10... | collective-permute-start | bytes 1474568 | tf_op jit(solution)/shard_map/ppermute | solution.py:582
  47.6 21.9 %collective-permute-start.11 = (bf16[256,768]{1,0:T(8,128)(2,1)S(1)}, bf16[256,768]{1,0:T(8,128)(2,1)}, u32[]{:S(2)}, u32[]{:S(2)}) collective-permute-start(bf16[256,768]{1,0:T(8,128)(2,1)S(1)} %bitcast.227), channel_id=1, source_target_pairs={{24,0},{0,8},{8,16},{16,24},{25,1},{1,9},{9,17},{17,25},{26,2},{2,... | collective-permute-start | bytes 1179656 | tf_op jit(solution)/shard_map/ppermute | solution.py:582
  69.5 23.9 %collective-permute-start.13 = (bf16[256,768]{1,0:T(8,128)(2,1)}, bf16[256,768]{1,0:T(8,128)(2,1)}, u32[]{:S(2)}, u32[]{:S(2)}) collective-permute-start(bf16[256,768]{1,0:T(8,128)(2,1)} %collective-permute-done.11.refs_1_.refs_3_), channel_id=1, source_target_pairs={{0,4},{4,0},{1,5},{5,1},{2,6},{6,2},{3,7},{7,3},{8,12},{12,8},{9,1... | collective-permute-start | bytes 1179656 | tf_op jit(solution)/shard_map/ppermute | solution.py:591
  70.5 22.8 %collective-permute-start.14 = (bf16[256,768]{1,0:T(8,128)(2,1)}, bf16[256,768]{1,0:T(8,128)(2,1)}, u32[]{:S(2)}, u32[]{:S(2)}) collective-permute-start(bf16[256,768]{1,0:T(8,128)(2,1)} %collective-permute-done.1.refs_1_.refs_3_), channel_id=1, source_target_pairs={{8,0},{16,8},{24,16},{0,24},{9,1},{17,9},{25,17},{1,25},{10,2},{18... | collective-permute-start | bytes 1179656 | tf_op jit(solution)/shard_map/ppermute | solution.py:582
  95.5 10.5 %collective-permute-start.15 = (bf16[2,256,768]{2,1,0:T(8,128)(2,1)}, bf16[2,256,768]{2,1,0:T(8,128)(2,1)}, u32[]{:S(2)}, u32[]{:S(2)}) collective-permute-start(bf16[2,256,768]{2,1,0:T(8,128)(2,1)} %pad_maximum_fusion.3), channel_id=1, source_target_pairs={{0,2},{2,0},{1,3},{3,1},{4,6},{6,4},{5,7},{7,5},{8,10},{10,8},{9,1... | collective-permute-start | bytes 2359304 | tf_op jit(solution)/shard_map/ppermute | solution.py:589
  95.6 12.5 %collective-permute-start.16 = (bf16[256,768]{1,0:T(8,128)(2,1)}, bf16[256,768]{1,0:T(8,128)(2,1)S(1)}, u32[]{:S(2)}, u32[]{:S(2)}) collective-permute-start(bf16[256,768]{1,0:T(8,128)(2,1)} %collective-permute-done.14.refs_1_.refs_3_), channel_id=1, source_target_pairs={{0,4},{4,0},{1,5},{5,1},{2,6},{6,2},{3,7},{7,3},{8,12},{12,8},{9,1... | collective-permute-start | bytes 1179656 | tf_op jit(solution)/shard_map/ppermute | solution.py:591
  172.8 22.5 %collective-permute-start.27 = (bf16[2,4,24,2304]{3,2,1,0:T(8,128)(2,1)S(1)}, bf16[2,4,24,2304]{3,2,1,0:T(8,128)(2,1)S(1)}, u32[]{:S(2)}, u32[]{:S(2)}) collective-permute-start(bf16[2,4,24,2304]{3,2,1,0:T(8,128)(2,1)S(1)} %fusion.4), channel_id=1, source_target_pairs={{1,0},{0,1},{3,2},{2,3},{5,4},{4,5},{7,6},{6,7},{9,8},{8,9},{11,10... | collective-permute-start | bytes 2654216 | tf_op jit(solution)/shard_map/ppermute | solution.py:582
  175.6 35.5 %collective-permute-start.31 = (bf16[2,4,24,1536]{3,2,1,0:T(8,128)(2,1)S(1)}, bf16[2,4,24,1536]{3,2,1,0:T(8,128)(2,1)S(1)}, u32[]{:S(2)}, u32[]{:S(2)}) collective-permute-start(bf16[2,4,24,1536]{3,2,1,0:T(8,128)(2,1)S(1)} %fusion.5), channel_id=1, source_target_pairs={{1,0},{0,1},{3,2},{2,3},{5,4},{4,5},{7,6},{6,7},{9,8},{8,9},{11,10... | collective-permute-start | bytes 1769480 | tf_op jit(solution)/shard_map/ppermute | solution.py:582
  196.9 14.2 %collective-permute-start.29 = (bf16[4,24,2304]{2,1,0:T(8,128)(2,1)S(1)}, bf16[4,24,2304]{2,1,0:T(8,128)(2,1)S(1)}, u32[]{:S(2)}, u32[]{:S(2)}) collective-permute-start(bf16[4,24,2304]{2,1,0:T(8,128)(2,1)S(1)} %fusion.8), channel_id=1, source_target_pairs={{4,0},{0,4},{5,1},{1,5},{6,2},{2,6},{7,3},{3,7},{12,8},{8,12},{13,... | collective-permute-start | bytes 1327112 | tf_op jit(solution)/shard_map/ppermute | solution.py:582
  198.8 19.2 %collective-permute-start.30 = (bf16[256,768]{1,0:T(8,128)(2,1)S(1)}, bf16[256,768]{1,0:T(8,128)(2,1)S(1)}, u32[]{:S(2)}, u32[]{:S(2)}) collective-permute-start(bf16[256,768]{1,0:T(8,128)(2,1)S(1)} %fusion.10), channel_id=1, source_target_pairs={{0,4},{4,0},{1,5},{5,1},{2,6},{6,2},{3,7},{7,3},{8,12},{12,8},{9,1... | collective-permute-start | bytes 1179656 | tf_op jit(solution)/shard_map/ppermute | solution.py:591
  218.3 33.1 %collective-permute-start.35 = (bf16[256,768]{1,0:T(8,128)(2,1)S(1)}, bf16[256,768]{1,0:T(8,128)(2,1)S(1)}, u32[]{:S(2)}, u32[]{:S(2)}) collective-permute-start(bf16[256,768]{1,0:T(8,128)(2,1)S(1)} %add_convert_fusion.5), channel_id=1, source_target_pairs={{24,0},{0,8},{8,16},{16,24},{25,1},{1,9},{9,17},{17,25},{26,2},{2,... | collective-permute-start | bytes 1179656 | tf_op jit(solution)/shard_map/ppermute | solution.py:582
  218.6 32.8 %collective-permute-start.34 = (bf16[2,24,2304]{2,1,0:T(8,128)(2,1)S(1)}, bf16[2,24,2304]{2,1,0:T(8,128)(2,1)S(1)}, u32[]{:S(2)}, u32[]{:S(2)}) collective-permute-start(bf16[2,24,2304]{2,1,0:T(8,128)(2,1)S(1)} %slice.343), channel_id=1, source_target_pairs={{0,16},{8,24},{16,0},{24,8},{1,17},{9,25},{17,1},{25,9},{2,18},{10... | collective-permute-start | bytes 663560 | tf_op jit(solution)/shard_map/ppermute | solution.py:647
  224.8 26.6 %collective-permute-start.33 = (bf16[4,24,1536]{2,1,0:T(8,128)(2,1)S(1)}, bf16[4,24,1536]{2,1,0:T(8,128)(2,1)S(1)}, u32[]{:S(2)}, u32[]{:S(2)}) collective-permute-start(bf16[4,24,1536]{2,1,0:T(8,128)(2,1)S(1)} %fusion.15), channel_id=1, source_target_pairs={{4,0},{0,4},{5,1},{1,5},{6,2},{2,6},{7,3},{3,7},{12,8},{8,12},{13,... | collective-permute-start | bytes 884744 | tf_op jit(solution)/shard_map/ppermute | solution.py:582
  226.6 24.8 %collective-permute-start.36 = (bf16[256,768]{1,0:T(8,128)(2,1)S(1)}, bf16[256,768]{1,0:T(8,128)(2,1)S(1)}, u32[]{:S(2)}, u32[]{:S(2)}) collective-permute-start(bf16[256,768]{1,0:T(8,128)(2,1)S(1)} %fusion.11), channel_id=1, source_target_pairs={{0,4},{4,0},{1,5},{5,1},{2,6},{6,2},{3,7},{7,3},{8,12},{12,8},{9,1... | collective-permute-start | bytes 1179656 | tf_op jit(solution)/shard_map/ppermute | solution.py:591
  253.4 25.1 %collective-permute-start.40 = (bf16[256,768]{1,0:T(8,128)(2,1)}, bf16[256,768]{1,0:T(8,128)(2,1)}, u32[]{:S(2)}, u32[]{:S(2)}) collective-permute-start(bf16[256,768]{1,0:T(8,128)(2,1)} %add_convert_fusion.4), channel_id=1, source_target_pairs={{8,0},{16,8},{24,16},{0,24},{9,1},{17,9},{25,17},{1,25},{10,2},{18... | collective-permute-start | bytes 1179656 | tf_op jit(solution)/shard_map/ppermute | solution.py:582
  254.7 23.7 %collective-permute-start.39 = (bf16[1,24,2304]{2,1,0:T(8,128)(2,1)}, bf16[1,24,2304]{2,1,0:T(8,128)(2,1)}, u32[]{:S(2)}, u32[]{:S(2)}) collective-permute-start(bf16[1,24,2304]{2,1,0:T(8,128)(2,1)} %slice.345), channel_id=1, source_target_pairs={{0,8},{8,0},{16,24},{24,16},{1,9},{9,1},{17,25},{25,17},{2,10},{10... | collective-permute-start | bytes 331784 | tf_op jit(solution)/shard_map/ppermute | solution.py:647
  255.6 22.8 %collective-permute-start.38 = (bf16[2,24,1536]{2,1,0:T(8,128)(2,1)S(1)}, bf16[2,24,1536]{2,1,0:T(8,128)(2,1)}, u32[]{:S(2)}, u32[]{:S(2)}) collective-permute-start(bf16[2,24,1536]{2,1,0:T(8,128)(2,1)S(1)} %slice.344), channel_id=1, source_target_pairs={{0,16},{8,24},{16,0},{24,8},{1,17},{9,25},{17,1},{25,9},{2,18},{10... | collective-permute-start | bytes 442376 | tf_op jit(solution)/shard_map/ppermute | solution.py:647
  257.1 21.3 %collective-permute-start.41 = (bf16[256,768]{1,0:T(8,128)(2,1)}, bf16[256,768]{1,0:T(8,128)(2,1)}, u32[]{:S(2)}, u32[]{:S(2)}) collective-permute-start(bf16[256,768]{1,0:T(8,128)(2,1)} %fusion.12), channel_id=1, source_target_pairs={{0,4},{4,0},{1,5},{5,1},{2,6},{6,2},{3,7},{7,3},{8,12},{12,8},{9,1... | collective-permute-start | bytes 1179656 | tf_op jit(solution)/shard_map/ppermute | solution.py:591
  276.9 19.2 %collective-permute-start.42 = (bf16[4,4,24,640]{3,2,1,0:T(8,128)(2,1)S(1)}, bf16[4,4,24,640]{3,2,1,0:T(8,128)(2,1)S(1)}, u32[]{:S(2)}, u32[]{:S(2)}) collective-permute-start(bf16[4,4,24,640]{3,2,1,0:T(8,128)(2,1)S(1)} %get-tuple-element.434), channel_id=1, source_target_pairs={{1,0},{0,1},{3,2},{2,3},{5,4},{4,5},{7,6},{6,7},{9,8},{8,9},{11,10... | collective-permute-start | bytes 1474568 | tf_op jit(solution)/shard_map/ppermute | solution.py:582
  279.6 16.5 %collective-permute-start.44 = (bf16[256,768]{1,0:T(8,128)(2,1)S(1)}, bf16[256,768]{1,0:T(8,128)(2,1)S(1)}, u32[]{:S(2)}, u32[]{:S(2)}) collective-permute-start(bf16[256,768]{1,0:T(8,128)(2,1)S(1)} %add_convert_fusion.3), channel_id=1, source_target_pairs={{24,0},{0,8},{8,16},{16,24},{25,1},{1,9},{9,17},{17,25},{26,2},{2,... | collective-permute-start | bytes 1179656 | tf_op jit(solution)/shard_map/ppermute | solution.py:582
  281.4 14.8 %collective-permute-start.45 = (bf16[2,256,768]{2,1,0:T(8,128)(2,1)S(1)}, bf16[2,256,768]{2,1,0:T(8,128)(2,1)S(1)}, u32[]{:S(2)}, u32[]{:S(2)}) collective-permute-start(bf16[2,256,768]{2,1,0:T(8,128)(2,1)S(1)} %get-tuple-element.395), channel_id=1, source_target_pairs={{0,2},{2,0},{1,3},{3,1},{4,6},{6,4},{5,7},{7,5},{8,10},{10,8},{9,1... | collective-permute-start | bytes 2359304 | tf_op jit(solution)/shard_map/ppermute | solution.py:589
  282.3 13.8 %collective-permute-start.43 = (bf16[1,24,1536]{2,1,0:T(8,128)(2,1)S(1)}, bf16[1,24,1536]{2,1,0:T(8,128)(2,1)S(1)}, u32[]{:S(2)}, u32[]{:S(2)}) collective-permute-start(bf16[1,24,1536]{2,1,0:T(8,128)(2,1)S(1)} %slice.346), channel_id=1, source_target_pairs={{0,8},{8,0},{16,24},{24,16},{1,9},{9,1},{17,25},{25,17},{2,10},{10... | collective-permute-start | bytes 221192 | tf_op jit(solution)/shard_map/ppermute | solution.py:647
  296.9 13.7 %collective-permute-start.49 = (bf16[256,768]{1,0:T(8,128)(2,1)S(1)}, bf16[256,768]{1,0:T(8,128)(2,1)}, u32[]{:S(2)}, u32[]{:S(2)}) collective-permute-start(bf16[256,768]{1,0:T(8,128)(2,1)S(1)} %fusion.13), channel_id=1, source_target_pairs={{0,4},{4,0},{1,5},{5,1},{2,6},{6,2},{3,7},{7,3},{8,12},{12,8},{9,1... | collective-permute-start | bytes 1179656 | tf_op jit(solution)/shard_map/ppermute | solution.py:591
  298.4 12.2 %collective-permute-start.47 = (bf16[4,24,640]{2,1,0:T(8,128)(2,1)S(1)}, bf16[4,24,640]{2,1,0:T(8,128)(2,1)S(1)}, u32[]{:S(2)}, u32[]{:S(2)}) collective-permute-start(bf16[4,24,640]{2,1,0:T(8,128)(2,1)S(1)} %get-tuple-element.432), channel_id=1, source_target_pairs={{16,0},{24,8},{0,16},{8,24},{17,1},{25,9},{1,17},{9,25},{18,2},{26... | collective-permute-start | bytes 368648 | tf_op jit(solution)/shard_map/ppermute | solution.py:582
  (70 other events, 422.3 us)
Sparse Core Ops, SparseCore 0:
  11.4 106.9 all-gather.1
  166.0 135.1 reduce-scatter.1
where the time goes:
time: 335 us; the launch traced here: 331 us
  Pallas kernels  103 us (31%)
  waiting for transfers between devices  99.2 us (30%)
  starting transfers between devices  56.5 us (17%)
  local copies, waits for them, and re-layouts  29.8 us (9%)
  other arithmetic  24.6 us (7%)
  between operations  17.2 us (5%)
    ppermute x18, waiting for transfers between devices, from_shift(): lax.ppermute(value, axis, [((i + step) % count, i) for i in range(count)])  54.4 us
    pallas_call x4, Pallas kernels, attend_back_chunk(): pl.pallas_call(partial(backward_kernel, first, last, min(256, rows), min(...  47.2 us
    pallas_call x4, Pallas kernels, attend_chunk(): pl.pallas_call(partial(forward_kernel, first, last, min(1024, rows), min(...  36.1 us
    ppermute x18, starting transfers between devices, from_shift(): lax.ppermute(value, axis, [((i + step) % count, i) for i in range(count)])  30.9 us
    ppermute x4, waiting for transfers between devices, over_q(): return (total[:half], lax.ppermute(total[half:].astype(bf16), 'q', pairs))  23.4 us
    pallas_call x1, Pallas kernels, ffn_block(): pl.pallas_call(partial(ffn_kernel, layout), out_shape=out_shape + targets...  18.8 us
    ppermute x12, starting transfers between devices, square_swap(): return lax.ppermute(value, 'x', [(0, 1), (1, 0)])  13.2 us
    ppermute x12, waiting for transfers between devices, square_swap(): return lax.ppermute(value, 'x', [(0, 1), (1, 0)])  12.8 us
  transfers between devices with their start and end apart: 55, of which 20 were waited for; matrix products, arithmetic and copies ran while one was open for 12% of the time, Pallas kernels for 25%

commit v1 on v0

--- a/solution.py
+++ b/solution.py
@@ -396,7 +396,7 @@
     out_ref, resid_ref = [refs.pop(0) for _ in range(2)]
     da_refs = [refs.pop(0) for _ in range(4)]
     vec_out = refs.pop(0)
-    targets = [refs.pop(0) for _ in range(5 if aligned else 1)]
+    targets = [refs.pop(0) for _ in range(3 if aligned else 1)]
     wo, w1, w2, go, g1, g2, act, slope, in_sem, out_sem = refs
     group, zi, xi, ci, bi, start, length = [where_ref[i] for i in range(7)]
     rows, width = x_ref.shape
@@ -503,8 +503,7 @@
 
 def unit_parts(fold):
     count = 1 + 2 * fold
-    edges = [0, count // 3, (count + 1) // 2, count]
-    return [range(edges[i], edges[i + 1]) for i in range(3)]
+    return [range(count // 3), range(count // 3, count)]
 
 
 def ffn_block(layout, where, att, x, cot, vectors, ebias, packed):
@@ -620,7 +619,7 @@
     return [from_shift(part, axis, count, count - j - 1) for j, part in enumerate(parts)]
 
 
-def weight_sum(keep, send, n_q, n_b, bi, order):
+def weight_sum(keep, send, n_q, n_b, bi):
     def own_b(keep, got, j):
         shape = (2, n_q, n_b, -1, keep.shape[-1])
         both = [pick(v.reshape(shape), (bi + j) % n_b, 2).astype(f32) for v in (keep, got)]
@@ -630,10 +629,7 @@
         return keep, square_swap(send, 1)
 
     def over_b(keep, got):
-        if order:
-            keep = lax.optimization_barrier((keep, order.pop()))[0]
         away = [own_b(keep, got, j).astype(bf16) for j in range(1, n_b)]
-        order.append(away[0])
         return keep, got, *[from_shift(v, "b", n_b, n_b - 1 - j) for j, v in enumerate(away)]
 
     def over_x(keep, got, *more):
@@ -839,13 +835,12 @@
     att_grads, vec_grads, summands = outs[2:6], outs[6], outs[7:]
     square = Chain(att_grads, lambda *parts: [square_swap(v, r) for r, v in enumerate(parts)])
 
-    sums, order = [], []
+    sums = []
     if aligned:
-        for i in range(2):
-            sums.append(weight_sum(summands[2 * i], summands[2 * i + 1], n_q, n_b, bi, order))
+        sums.append(weight_sum(summands[0], summands[1], n_q, n_b, bi))
     reduced = lax.psum_scatter(summands[-1], AXES, scatter_dimension=0, tiled=True)
     run_stage([square] + sums)
-    plan = [([0], [], [1]), ([0], [1], []), ([1, 0], [], []), ([1, 0], [], [])]
+    plan = [([0], [], [])] * 4
     shared = (qx2, qp, w_own, square.state, attx)
     carry = None
     moving, moving_to = [], {}
@@ -901,7 +896,7 @@
     rows = Chain((total,), rows_over_b, rows_over_q, rows_over_square)
     while any(c.steps for c in [rows, *sums, *moving]):
         run_stage([c for c in [rows, *sums, *moving] if c.steps])
-        if len(rows.steps) == 1:
+        if not rows.steps:
             reduced, rows.state = lax.optimization_barrier((reduced, rows.state))
     summed = reduced.astype(f32)
     token_grad = resid_first_grad

time: 335 us -> 333 us (level)
  waiting for transfers between devices: 99.2 us -> 109 us
  other arithmetic: 24.6 us -> 18.6 us
  local copies, waits for them, and re-layouts: 29.8 us -> 26.4 us
    ppermute x18 -> x16, waiting for transfers between devices: 54.4 us -> 67.3 us  [from_shift(): lax.ppermute(value, axis, [((i + step) % count, i) for i in range(count)])]
    ppermute x4 -> x2, waiting for transfers between devices: 23.4 us -> 18.7 us  [over_q(): return (total[:half], lax.ppermute(total[half:].astype(bf16), 'q', pairs))]
    ppermute x4 -> x2, starting transfers between devices: 7.86 us -> 4.85 us  [over_q(): return (total[:half], lax.ppermute(total[half:].astype(bf16), 'q', pairs))]
    ppermute x18 -> x16, starting transfers between devices: 30.9 us -> 32.3 us  [from_shift(): lax.ppermute(value, axis, [((i + step) % count, i) for i in range(count)])]
    unnamed x95 -> x83, local copies, waits for them, and re-layouts: 7.95 us -> 8.27 us
  transfers between devices with their start and end apart: 55 -> 50, of which waited for: 20 -> 23; matrix products, arithmetic and copies ran while one was open for 12% -> 9% of each run, Pallas kernels for 25% -> 25%
where the time goes in v1:
time: 333 us; the launch traced here: 329 us
  waiting for transfers between devices  109 us (33%)
  Pallas kernels  103 us (31%)
  starting transfers between devices  54.8 us (16%)
  local copies, waits for them, and re-layouts  26.4 us (8%)
  other arithmetic  18.6 us (6%)
  between operations  16.6 us (5%)
    ppermute x16, waiting for transfers between devices, from_shift(): lax.ppermute(value, axis, [((i + step) % count, i) for i in range(count)])  67.3 us
    pallas_call x4, Pallas kernels, attend_back_chunk(): pl.pallas_call(partial(backward_kernel, first, last, min(256, rows), min(...  47.2 us
    pallas_call x4, Pallas kernels, attend_chunk(): pl.pallas_call(partial(forward_kernel, first, last, min(1024, rows), min(...  36.1 us
    ppermute x16, starting transfers between devices, from_shift(): lax.ppermute(value, axis, [((i + step) % count, i) for i in range(count)])  32.3 us
    pallas_call x1, Pallas kernels, ffn_block(): pl.pallas_call(partial(ffn_kernel, layout), out_shape=out_shape + targets...  18.9 us
    ppermute x2, waiting for transfers between devices, over_q(): return (total[:half], lax.ppermute(total[half:].astype(bf16), 'q', pairs))  18.7 us
    ppermute x12, starting transfers between devices, square_swap(): return lax.ppermute(value, 'x', [(0, 1), (1, 0)])  13.9 us
    ppermute x12, waiting for transfers between devices, square_swap(): return lax.ppermute(value, 'x', [(0, 1), (1, 0)])  13 us
  transfers between devices with their start and end apart: 50, of which 23 were waited for; matrix products, arithmetic and copies ran while one was open for 9% of the time, Pallas kernels for 25%

profile of v1, /device:TPU:0, one launch (start us, length us, event | category | flops | bytes accessed | tf_op | source)
XLA Modules:
  0.0 329.2 jit_solution(17217371239229230225)
XLA Ops:
  10.1 3.0 collective-permute-start
  13.1 3.6 %collective-permute-start.1 = (bf16[256,768]{1,0:T(8,128)(2,1)S(1)}, bf16[256,768]{1,0:T(8,128)(2,1)}, u32[]{:S(2)}, u32[]{:S(2)}) collective-permute-start(bf16[256,768]{1,0:T(8,128)(2,1)S(1)} %bitcast.208), channel_id=1, source_target_pairs={{8,0},{16,8},{24,16},{0,24},{9,1},{17,9},{25,17},{1,25},{10,2},{18... | collective-permute-start | bytes 1179656 | tf_op jit(solution)/shard_map/ppermute | solution.py:581
  20.7 2.4 collective-permute-done.3
  23.3 4.0 %collective-permute-done.1.refs_1_.refs_3_ = bf16[256,768]{1,0:T(8,128)(2,1)} collective-permute-done((bf16[256,768]{1,0:T(8,128)(2,1)S(1)}, bf16[256,768]{1,0:T(8,128)(2,1)}, u32[]{:S(2)}, u32[]{:S(2)}) %collective-permute-start.1) | collective-permute-done | bytes 393248 | tf_op jit(solution)/shard_map/ppermute | solution.py:581
  27.6 4.4 %collective-permute-start.7 = (bf16[4,24,640]{2,1,0:T(8,128)(2,1)S(1)}, bf16[4,24,640]{2,1,0:T(8,128)(2,1)S(1)}, u32[]{:S(2)}, u32[]{:S(2)}) collective-permute-start(bf16[4,24,640]{2,1,0:T(8,128)(2,1)S(1)} %pad_maximum_fusion.8), channel_id=1, source_target_pairs={{8,0},{16,8},{24,16},{0,24},{9,1},{17,9},{25,17},{1,25},{10,2},{18... | collective-permute-start | bytes 368648 | tf_op jit(solution)/shard_map/ppermute | solution.py:581
  33.6 5.4 %collective-permute-done.7 = bf16[4,24,640]{2,1,0:T(8,128)(2,1)S(1)} collective-permute-done((bf16[4,24,640]{2,1,0:T(8,128)(2,1)S(1)}, bf16[4,24,640]{2,1,0:T(8,128)(2,1)S(1)}, u32[]{:S(2)}, u32[]{:S(2)}) %collective-permute-start.7) | collective-permute-done | bytes 122912 | tf_op jit(solution)/shard_map/ppermute | solution.py:581
  39.0 5.6 %collective-permute-done.8 = bf16[4,24,640]{2,1,0:T(8,128)(2,1)S(1)} collective-permute-done((bf16[4,24,640]{2,1,0:T(8,128)(2,1)S(1)}, bf16[4,24,640]{2,1,0:T(8,128)(2,1)S(1)}, u32[]{:S(2)}, u32[]{:S(2)}) %collective-permute-start.8) | collective-permute-done | bytes 122912 | tf_op jit(solution)/shard_map/ppermute | solution.py:581
  50.2 19.3 %collective-permute-done.11.refs_1_.refs_3_ = bf16[256,768]{1,0:T(8,128)(2,1)} collective-permute-done((bf16[256,768]{1,0:T(8,128)(2,1)S(1)}, bf16[256,768]{1,0:T(8,128)(2,1)}, u32[]{:S(2)}, u32[]{:S(2)}) %collective-permute-start.11) | collective-permute-done | bytes 393248 | tf_op jit(solution)/shard_map/ppermute | solution.py:581
  70.5 5.8 %collective-permute-start.14 = (bf16[256,768]{1,0:T(8,128)(2,1)}, bf16[256,768]{1,0:T(8,128)(2,1)}, u32[]{:S(2)}, u32[]{:S(2)}) collective-permute-start(bf16[256,768]{1,0:T(8,128)(2,1)} %collective-permute-done.1.refs_1_.refs_3_), channel_id=1, source_target_pairs={{8,0},{16,8},{24,16},{0,24},{9,1},{17,9},{25,17},{1,25},{10,2},{18... | collective-permute-start | bytes 1179656 | tf_op jit(solution)/shard_map/ppermute | solution.py:581
  78.1 8.6 %attend_forward.4 = (bf16[3,1024,256]{2,1,0:T(8,128)(2,1)}, bf16[3,1024,128]{2,1,0:T(8,128)(2,1)}, bf16[3,1024,256]{2,1,0:T(8,128)(2,1)S(1)}, bf16[3,1024,128]{2...) custom-call(s32[5]{0:T(128)S(1)} %stack.273.refs_0_, bf16[256,768]{1,0:T(8,128)(2,1)} %bitcast.205, ...), custom_call_target="tpu_custom_call" | custom-call | flops 8000000000 | bytes 10000000 | tf_op jit(solution)/shard_map/attend_forward/pallas_call | solution.py:190
  88.6 4.8 %collective-permute-done.14.refs_1_.refs_3_ = bf16[256,768]{1,0:T(8,128)(2,1)} collective-permute-done((bf16[256,768]{1,0:T(8,128)(2,1)}, bf16[256,768]{1,0:T(8,128)(2,1)}, u32[]{:S(2)}, u32[]{:S(2)}) %collective-permute-start.14) | collective-permute-done | bytes 393248 | tf_op jit(solution)/shard_map/ppermute | solution.py:581
  96.8 9.2 %attend_forward.5 = (bf16[3,1024,256]{2,1,0:T(8,128)(2,1)}, bf16[3,1024,128]{2,1,0:T(8,128)(2,1)}, f32[3,8,1024]{2,1,0:T(8,128)S(1)}, f32[3,80,1024]{2,1,0:T(8,128)S(1)}) custom-call(s32[5]{0:T(128)S(1)} %stack.240.refs_0_, bf16[256,768]{1,0:T(8,128)(2,1)} %collective-permute-done.1.refs_1_.refs_3_, bf16[256,768]{1,0:T(8,128)(2,1)} %get-tuple-element.219.refs_2_.refs_4_, ...), custom_call_target="tpu_custom_call" | custom-call | flops 8000000000 | bytes 10000000 | tf_op jit(solution)/shard_map/attend_forward/pallas_call | solution.py:190
  110.8 9.2 %attend_forward.6 = (bf16[3,1024,256]{2,1,0:T(8,128)(2,1)}, bf16[3,1024,128]{2,1,0:T(8,128)(2,1)}, f32[3,8,1024]{2,1,0:T(8,128)S(1)}, f32[3,80,1024]{2,1,0:T(8,128)S(1)}) custom-call(s32[5]{0:T(128)S(1)} %stack.235.refs_0_, bf16[256,768]{1,0:T(8,128)(2,1)} %collective-permute-done.11.refs_1_.refs_3_, bf16[256,768]{1,0:T(8,128)(2,1)} %get-tuple-element.247.refs_2_.refs_4_, ...), custom_call_target="tpu_custom_call" | custom-call | flops 8000000000 | bytes 10000000 | tf_op jit(solution)/shard_map/attend_forward/pallas_call | solution.py:190
  122.2 9.1 %attend_forward.7 = (bf16[3,1024,256]{2,1,0:T(8,128)(2,1)}, bf16[3,1024,128]{2,1,0:T(8,128)(2,1)}, bf16[256,192]{1,0:T(8,128)(2,1)S(1)}, bf16[256,192]{1,0:T(8,1...) custom-call(s32[5]{0:T(128)S(1)} %stack.230.refs_0_, ...), custom_call_target="tpu_custom_call" | custom-call | flops 8000000000 | bytes 10000000 | tf_op jit(solution)/shard_map/attend_forward/pallas_call | solution.py:190
  136.2 3.9 %collective-permute-done.18.refs_2_ = bf16[256,192]{1,0:T(8,128)(2,1)S(1)} collective-permute-done((bf16[256,192]{1,0:T(8,128)(2,1)S(1)}, bf16[256,192]{1,0:T(8,128)(2,1)S(1)}, u32[]{:S(2)}, u32[]{:S(2)}) %collective-permute-start.18) | collective-permute-done | bytes 98336 | tf_op jit(solution)/shard_map/ppermute | solution.py:588
  143.2 18.9 %feed_forward.1 = (bf16[256,768]{1,0:T(8,128)(2,1)}, f32[256,768]{1,0:T(8,128)S(1)}, bf16[256,192]{1,0:T(8,128)(2,1)S(1)}, bf16[256,192]{1,0:T(8,128)(2,1)S(1)},...) custom-call(s32[7]{0:T(128)S(1)} %stack.225.refs_0_, ...), custom_call_target="tpu_custom_call" | custom-call | flops 20000000000 | bytes 30000000 | tf_op jit(solution)/shard_map/feed_forward/pallas_call | solution.py:534
  165.8 3.2 collective-permute-done.23.refs_11_
  175.2 11.9 %attend_backward.4 = (bf16[2,256,768]{2,1,0:T(8,128)(2,1)S(1)}, bf16[2,256,768]{2,1,0:T(8,128)(2,1)S(1)}, bf16[3,1024,128]{2,1,0:T(8,128)(2,1)S(1)}, f32[3,64,10...) custom-call(bf16[3,1024,256]{2,1,0:T(8,128)(2,1)} %get-tuple-element.279.refs_0_, ...), custom_call_target="tpu_custom_call" | custom-call | flops 15000000512 | bytes 10000000 | tf_op jit(solution)/shard_map/attend_backward/pallas_call | solution.py:356
  187.1 7.3 %collective-permute-done.26 = bf16[2,4,24,2304]{3,2,1,0:T(8,128)(2,1)S(1)} collective-permute-done((bf16[2,4,24,2304]{3,2,1,0:T(8,128)(2,1)S(1)}, bf16[2,4,24,2304]{3,2,1,0:T(8,128)(2,1)S(1)}, u32[]{:S(2)}, u32[]{:S(2)}) %collective-permute-start.26) | collective-permute-done | bytes 884768 | tf_op jit(solution)/shard_map/ppermute | solution.py:581
  198.7 11.6 %attend_backward.5 = (bf16[2,256,768]{2,1,0:T(8,128)(2,1)S(1)}, bf16[2,256,768]{2,1,0:T(8,128)(2,1)S(1)}, f32[3,64,1024]{2,1,0:T(8,128)S(1)}, f32[768,512]{1,0:T(8,128)S(1)}, f32[8,512]{1,0:T(8,128)S(1)}) custom-call(bf16[3,1024,256]{2,1,0:T(8,128)(2,1)} %get-tuple-element.303.refs_0_, bf16[3,1024,128]{2,1,0:T(8,128)(2,1)} %get-tuple-element.304.refs_1_, ...), custom_call_target="tpu_custom_call" | custom-call | flops 15000000512 | bytes 10000000 | tf_op jit(solution)/shard_map/attend_backward/pallas_call | solution.py:356
  210.4 6.7 %collective-permute-done.29 = bf16[256,768]{1,0:T(8,128)(2,1)S(1)} collective-permute-done((bf16[256,768]{1,0:T(8,128)(2,1)S(1)}, bf16[256,768]{1,0:T(8,128)(2,1)S(1)}, u32[]{:S(2)}, u32[]{:S(2)}) %collective-permute-start.29) | collective-permute-done | bytes 393248 | tf_op jit(solution)/shard_map/ppermute | solution.py:590
  217.9 4.8 %collective-permute-start.31 = (bf16[2,24,2304]{2,1,0:T(8,128)(2,1)S(1)}, bf16[2,24,2304]{2,1,0:T(8,128)(2,1)S(1)}, u32[]{:S(2)}, u32[]{:S(2)}) collective-permute-start(bf16[2,24,2304]{2,1,0:T(8,128)(2,1)S(1)} %slice.302), channel_id=1, source_target_pairs={{0,16},{8,24},{16,0},{24,8},{1,17},{9,25},{17,1},{25,9},{2,18},{10... | collective-permute-start | bytes 663560 | tf_op jit(solution)/shard_map/ppermute | solution.py:643
  224.5 11.4 %attend_backward.6 = (bf16[2,256,768]{2,1,0:T(8,128)(2,1)S(1)}, bf16[2,256,768]{2,1,0:T(8,128)(2,1)S(1)}, f32[3,64,1024]{2,1,0:T(8,128)S(1)}, f32[768,512]{1,0:T(8,128)S(1)}, f32[8,512]{1,0:T(8,128)S(1)}) custom-call(bf16[3,1024,256]{2,1,0:T(8,128)(2,1)} %get-tuple-element.301.refs_0_, bf16[3,1024,128]{2,1,0:T(8,128)(2,1)} %get-tuple-element.302.refs_1_, ...), custom_call_target="tpu_custom_call" | custom-call | flops 15000000512 | bytes 10000000 | tf_op jit(solution)/shard_map/attend_backward/pallas_call | solution.py:356
  236.0 18.7 %collective-permute-done.31 = bf16[2,24,2304]{2,1,0:T(8,128)(2,1)S(1)} collective-permute-done((bf16[2,24,2304]{2,1,0:T(8,128)(2,1)S(1)}, bf16[2,24,2304]{2,1,0:T(8,128)(2,1)S(1)}, u32[]{:S(2)}, u32[]{:S(2)}) %collective-permute-start.31) | collective-permute-done | bytes 221216 | tf_op jit(solution)/shard_map/ppermute | solution.py:643
  255.8 3.8 %collective-permute-start.36 = (bf16[256,768]{1,0:T(8,128)(2,1)}, bf16[256,768]{1,0:T(8,128)(2,1)}, u32[]{:S(2)}, u32[]{:S(2)}) collective-permute-start(bf16[256,768]{1,0:T(8,128)(2,1)} %add_convert_fusion.3), channel_id=1, source_target_pairs={{8,0},{16,8},{24,16},{0,24},{9,1},{17,9},{25,17},{1,25},{10,2},{18... | collective-permute-start | bytes 1179656 | tf_op jit(solution)/shard_map/ppermute | solution.py:581
  263.1 12.2 %attend_backward.7 = (bf16[2,256,768]{2,1,0:T(8,128)(2,1)S(1)}, bf16[2,256,768]{2,1,0:T(8,128)(2,1)S(1)}, bf16[768,640]{1,0:T(8,128)(2,1)S(1)}, f32[8,640]{1,0:T(8,128)S(1)}) custom-call(bf16[3,1024,256]{2,1,0:T(8,128)(2,1)} %get-tuple-element.275.refs_0_, bf16[3,1024,128]{2,1,0:T(8,128)(2,1)} %get-tuple-element.276.refs_1_, bf16[768,640]{1,0:T(8,128)(2,1)} %copy-done, ...), custom_call_target="tpu_custom_call" | custom-call | flops 15000000512 | bytes 10000000 | tf_op jit(solution)/shard_map/attend_backward/pallas_call | solution.py:356
  281.2 2.4 collective-permute-start.39
  284.5 7.7 %collective-permute-done.38 = bf16[4,4,24,640]{3,2,1,0:T(8,128)(2,1)S(1)} collective-permute-done((bf16[4,4,24,640]{3,2,1,0:T(8,128)(2,1)S(1)}, bf16[4,4,24,640]{3,2,1,0:T(8,128)(2,1)S(1)}, u32[]{:S(2)}, u32[]{:S(2)}) %collective-permute-start.38) | collective-permute-done | bytes 491552 | tf_op jit(solution)/shard_map/ppermute | solution.py:581
  292.2 4.4 %collective-permute-done.39 = bf16[256,768]{1,0:T(8,128)(2,1)S(1)} collective-permute-done((bf16[256,768]{1,0:T(8,128)(2,1)S(1)}, bf16[256,768]{1,0:T(8,128)(2,1)S(1)}, u32[]{:S(2)}, u32[]{:S(2)}) %collective-permute-start.39) | collective-permute-done | bytes 393248 | tf_op jit(solution)/shard_map/ppermute | solution.py:581
  297.4 3.6 %collective-permute-start.43 = (bf16[4,24,640]{2,1,0:T(8,128)(2,1)S(1)}, bf16[4,24,640]{2,1,0:T(8,128)(2,1)S(1)}, u32[]{:S(2)}, u32[]{:S(2)}) collective-permute-start(bf16[4,24,640]{2,1,0:T(8,128)(2,1)S(1)} %get-tuple-element.403), channel_id=1, source_target_pairs={{8,0},{16,8},{24,16},{0,24},{9,1},{17,9},{25,17},{1,25},{10,2},{18... | collective-permute-start | bytes 368648 | tf_op jit(solution)/shard_map/ppermute | solution.py:581
  301.1 4.2 %collective-permute-done.41 = bf16[4,24,640]{2,1,0:T(8,128)(2,1)S(1)} collective-permute-done((bf16[4,24,640]{2,1,0:T(8,128)(2,1)S(1)}, bf16[4,24,640]{2,1,0:T(8,128)(2,1)S(1)}, u32[]{:S(2)}, u32[]{:S(2)}) %collective-permute-start.41) | collective-permute-done | bytes 122912 | tf_op jit(solution)/shard_map/ppermute | solution.py:581
  305.3 4.6 %collective-permute-done.42 = bf16[4,24,640]{2,1,0:T(8,128)(2,1)S(1)} collective-permute-done((bf16[4,24,640]{2,1,0:T(8,128)(2,1)S(1)}, bf16[4,24,640]{2,1,0:T(8,128)(2,1)S(1)}, u32[]{:S(2)}, u32[]{:S(2)}) %collective-permute-start.42) | collective-permute-done | bytes 122912 | tf_op jit(solution)/shard_map/ppermute | solution.py:581
  (297 shorter events, 76.8 us)
Async XLA Ops:
  7.2 126.7 %all-gather.2.cloned.1.call-start = ((), (), s32[]{:S(2)}) async-start(), calls=%async_computation.1 | async-start | bytes 5640192 | tf_op jit(solution)/shard_map/all_gather | solution.py:722
  10.0 304.8 %reduce-scatter.2.cloned.1.call-start = ((), (), s32[]{:S(2)}) async-start(), calls=%async_computation.2 | async-start | bytes 7299072 | tf_op jit(solution)/shard_map/reduce_scatter | solution.py:841
  10.1 13.2 %collective-permute-start = (bf16[256,768]{1,0:T(8,128)(2,1)S(1)}, bf16[256,768]{1,0:T(8,128)(2,1)S(1)}, u32[]{:S(2)}, u32[]{:S(2)}) collective-permute-start(bf16[256,768]{1,0:T(8,128)(2,1)S(1)} %bitcast.207), channel_id=1, source_target_pairs={{0,4},{4,0},{1,5},{5,1},{2,6},{6,2},{3,7},{7,3},{8,12},{12,8},{9,1... | collective-permute-start | bytes 1179656 | tf_op jit(solution)/shard_map/ppermute | solution.py:590
  13.1 14.2 %collective-permute-start.1 = (bf16[256,768]{1,0:T(8,128)(2,1)S(1)}, bf16[256,768]{1,0:T(8,128)(2,1)}, u32[]{:S(2)}, u32[]{:S(2)}) collective-permute-start(bf16[256,768]{1,0:T(8,128)(2,1)S(1)} %bitcast.208), channel_id=1, source_target_pairs={{8,0},{16,8},{24,16},{0,24},{9,1},{17,9},{25,17},{1,25},{10,2},{18... | collective-permute-start | bytes 1179656 | tf_op jit(solution)/shard_map/ppermute | solution.py:581
  27.5 17.2 %collective-permute-start.6 = (bf16[256,768]{1,0:T(8,128)(2,1)}, bf16[256,768]{1,0:T(8,128)(2,1)S(1)}, u32[]{:S(2)}, u32[]{:S(2)}) collective-permute-start(bf16[256,768]{1,0:T(8,128)(2,1)} %collective-permute-done.1.refs_1_.refs_3_), channel_id=1, source_target_pairs={{0,4},{4,0},{1,5},{5,1},{2,6},{6,2},{3,7},{7,3},{8,12},{12,8},{9,1... | collective-permute-start | bytes 1179656 | tf_op jit(solution)/shard_map/ppermute | solution.py:590
  27.6 11.5 %collective-permute-start.7 = (bf16[4,24,640]{2,1,0:T(8,128)(2,1)S(1)}, bf16[4,24,640]{2,1,0:T(8,128)(2,1)S(1)}, u32[]{:S(2)}, u32[]{:S(2)}) collective-permute-start(bf16[4,24,640]{2,1,0:T(8,128)(2,1)S(1)} %pad_maximum_fusion.8), channel_id=1, source_target_pairs={{8,0},{16,8},{24,16},{0,24},{9,1},{17,9},{25,17},{1,25},{10,2},{18... | collective-permute-start | bytes 368648 | tf_op jit(solution)/shard_map/ppermute | solution.py:581
  32.0 12.6 %collective-permute-start.8 = (bf16[4,24,640]{2,1,0:T(8,128)(2,1)S(1)}, bf16[4,24,640]{2,1,0:T(8,128)(2,1)S(1)}, u32[]{:S(2)}, u32[]{:S(2)}) collective-permute-start(bf16[4,24,640]{2,1,0:T(8,128)(2,1)S(1)} %pad_maximum_fusion.8), channel_id=1, source_target_pairs={{16,0},{24,8},{0,16},{8,24},{17,1},{25,9},{1,17},{9,25},{18,2},{26... | collective-permute-start | bytes 368648 | tf_op jit(solution)/shard_map/ppermute | solution.py:581
  32.0 12.6 %collective-permute-start.9 = (bf16[4,24,640]{2,1,0:T(8,128)(2,1)S(1)}, bf16[4,24,640]{2,1,0:T(8,128)(2,1)S(1)}, u32[]{:S(2)}, u32[]{:S(2)}) collective-permute-start(bf16[4,24,640]{2,1,0:T(8,128)(2,1)S(1)} %pad_maximum_fusion.8), channel_id=1, source_target_pairs={{24,0},{0,8},{8,16},{16,24},{25,1},{1,9},{9,17},{17,25},{26,2},{2,... | collective-permute-start | bytes 368648 | tf_op jit(solution)/shard_map/ppermute | solution.py:581
  46.0 23.4 %collective-permute-start.12 = (bf16[4,4,24,640]{3,2,1,0:T(8,128)(2,1)S(1)}, bf16[4,4,24,640]{3,2,1,0:T(8,128)(2,1)S(1)}, u32[]{:S(2)}, u32[]{:S(2)}) collective-permute-start(bf16[4,4,24,640]{3,2,1,0:T(8,128)(2,1)S(1)} %pad_maximum_fusion.5), channel_id=1, source_target_pairs={{1,0},{0,1},{3,2},{2,3},{5,4},{4,5},{7,6},{6,7},{9,8},{8,9},{11,10... | collective-permute-start | bytes 1474568 | tf_op jit(solution)/shard_map/ppermute | solution.py:581
  47.6 21.9 %collective-permute-start.11 = (bf16[256,768]{1,0:T(8,128)(2,1)S(1)}, bf16[256,768]{1,0:T(8,128)(2,1)}, u32[]{:S(2)}, u32[]{:S(2)}) collective-permute-start(bf16[256,768]{1,0:T(8,128)(2,1)S(1)} %bitcast.209), channel_id=1, source_target_pairs={{24,0},{0,8},{8,16},{16,24},{25,1},{1,9},{9,17},{17,25},{26,2},{2,... | collective-permute-start | bytes 1179656 | tf_op jit(solution)/shard_map/ppermute | solution.py:581
  69.5 23.9 %collective-permute-start.13 = (bf16[256,768]{1,0:T(8,128)(2,1)}, bf16[256,768]{1,0:T(8,128)(2,1)}, u32[]{:S(2)}, u32[]{:S(2)}) collective-permute-start(bf16[256,768]{1,0:T(8,128)(2,1)} %collective-permute-done.11.refs_1_.refs_3_), channel_id=1, source_target_pairs={{0,4},{4,0},{1,5},{5,1},{2,6},{6,2},{3,7},{7,3},{8,12},{12,8},{9,1... | collective-permute-start | bytes 1179656 | tf_op jit(solution)/shard_map/ppermute | solution.py:590
  70.5 22.8 %collective-permute-start.14 = (bf16[256,768]{1,0:T(8,128)(2,1)}, bf16[256,768]{1,0:T(8,128)(2,1)}, u32[]{:S(2)}, u32[]{:S(2)}) collective-permute-start(bf16[256,768]{1,0:T(8,128)(2,1)} %collective-permute-done.1.refs_1_.refs_3_), channel_id=1, source_target_pairs={{8,0},{16,8},{24,16},{0,24},{9,1},{17,9},{25,17},{1,25},{10,2},{18... | collective-permute-start | bytes 1179656 | tf_op jit(solution)/shard_map/ppermute | solution.py:581
  95.5 10.5 %collective-permute-start.15 = (bf16[2,256,768]{2,1,0:T(8,128)(2,1)}, bf16[2,256,768]{2,1,0:T(8,128)(2,1)}, u32[]{:S(2)}, u32[]{:S(2)}) collective-permute-start(bf16[2,256,768]{2,1,0:T(8,128)(2,1)} %pad_maximum_fusion.3), channel_id=1, source_target_pairs={{0,2},{2,0},{1,3},{3,1},{4,6},{6,4},{5,7},{7,5},{8,10},{10,8},{9,1... | collective-permute-start | bytes 2359304 | tf_op jit(solution)/shard_map/ppermute | solution.py:588
  95.5 12.5 %collective-permute-start.16 = (bf16[256,768]{1,0:T(8,128)(2,1)}, bf16[256,768]{1,0:T(8,128)(2,1)S(1)}, u32[]{:S(2)}, u32[]{:S(2)}) collective-permute-start(bf16[256,768]{1,0:T(8,128)(2,1)} %collective-permute-done.14.refs_1_.refs_3_), channel_id=1, source_target_pairs={{0,4},{4,0},{1,5},{5,1},{2,6},{6,2},{3,7},{7,3},{8,12},{12,8},{9,1... | collective-permute-start | bytes 1179656 | tf_op jit(solution)/shard_map/ppermute | solution.py:590
  110.1 9.9 %collective-permute-start.17 = (bf16[2,256,768]{2,1,0:T(8,128)(2,1)}, bf16[2,256,768]{2,1,0:T(8,128)(2,1)}, u32[]{:S(2)}, u32[]{:S(2)}) collective-permute-start(bf16[2,256,768]{2,1,0:T(8,128)(2,1)} %pad_maximum_fusion.4), channel_id=1, source_target_pairs={{0,2},{2,0},{1,3},{3,1},{4,6},{6,4},{5,7},{7,5},{8,10},{10,8},{9,1... | collective-permute-start | bytes 2359304 | tf_op jit(solution)/shard_map/ppermute | solution.py:588
  133.9 9.3 %collective-permute-start.21 = (bf16[384,6912]{1,0:T(8,128)(2,1)}, bf16[384,6912]{1,0:T(8,128)(2,1)}, u32[]{:S(2)}, u32[]{:S(2)}) collective-permute-start(bf16[384,6912]{1,0:T(8,128)(2,1)} %all-gather.2.cloned.1.call-done.refs_9_), channel_id=1, source_target_pairs={{0,2},{2,0},{1,3},{3,1},{4,6},{6,4},{5,7},{7,5},{8,10},{10,8},{9,1... | collective-permute-start | bytes 15925256 | tf_op jit(solution)/shard_map/ppermute | solution.py:588
  162.1 8.4 %collective-permute-start.25 = (bf16[2,4,48,2304]{3,2,1,0:T(8,128)(2,1)}, bf16[2,4,48,2304]{3,2,1,0:T(8,128)(2,1)}, u32[]{:S(2)}, u32[]{:S(2)}) collective-permute-start(bf16[2,4,48,2304]{3,2,1,0:T(8,128)(2,1)} %get-tuple-element.286), channel_id=1, source_target_pairs={{0,2},{2,0},{1,3},{3,1},{4,6},{6,4},{5,7},{7,5},{8,10},{10,8},{9,1... | collective-permute-start | bytes 5308424 | tf_op jit(solution)/shard_map/ppermute | solution.py:588
  172.3 22.1 %collective-permute-start.26 = (bf16[2,4,24,2304]{3,2,1,0:T(8,128)(2,1)S(1)}, bf16[2,4,24,2304]{3,2,1,0:T(8,128)(2,1)S(1)}, u32[]{:S(2)}, u32[]{:S(2)}) collective-permute-start(bf16[2,4,24,2304]{3,2,1,0:T(8,128)(2,1)S(1)} %fusion.4), channel_id=1, source_target_pairs={{1,0},{0,1},{3,2},{2,3},{5,4},{4,5},{7,6},{6,7},{9,8},{8,9},{11,10... | collective-permute-start | bytes 2654216 | tf_op jit(solution)/shard_map/ppermute | solution.py:581
  196.0 14.4 %collective-permute-start.28 = (bf16[4,24,2304]{2,1,0:T(8,128)(2,1)S(1)}, bf16[4,24,2304]{2,1,0:T(8,128)(2,1)S(1)}, u32[]{:S(2)}, u32[]{:S(2)}) collective-permute-start(bf16[4,24,2304]{2,1,0:T(8,128)(2,1)S(1)} %fusion.7), channel_id=1, source_target_pairs={{4,0},{0,4},{5,1},{1,5},{6,2},{2,6},{7,3},{3,7},{12,8},{8,12},{13,... | collective-permute-start | bytes 1327112 | tf_op jit(solution)/shard_map/ppermute | solution.py:581
  198.1 19.0 %collective-permute-start.29 = (bf16[256,768]{1,0:T(8,128)(2,1)S(1)}, bf16[256,768]{1,0:T(8,128)(2,1)S(1)}, u32[]{:S(2)}, u32[]{:S(2)}) collective-permute-start(bf16[256,768]{1,0:T(8,128)(2,1)S(1)} %fusion.9), channel_id=1, source_target_pairs={{0,4},{4,0},{1,5},{5,1},{2,6},{6,2},{3,7},{7,3},{8,12},{12,8},{9,1... | collective-permute-start | bytes 1179656 | tf_op jit(solution)/shard_map/ppermute | solution.py:590
  217.2 37.4 %collective-permute-start.32 = (bf16[256,768]{1,0:T(8,128)(2,1)S(1)}, bf16[256,768]{1,0:T(8,128)(2,1)S(1)}, u32[]{:S(2)}, u32[]{:S(2)}) collective-permute-start(bf16[256,768]{1,0:T(8,128)(2,1)S(1)} %add_convert_fusion.4), channel_id=1, source_target_pairs={{24,0},{0,8},{8,16},{16,24},{25,1},{1,9},{9,17},{17,25},{26,2},{2,... | collective-permute-start | bytes 1179656 | tf_op jit(solution)/shard_map/ppermute | solution.py:581
  217.9 36.7 %collective-permute-start.31 = (bf16[2,24,2304]{2,1,0:T(8,128)(2,1)S(1)}, bf16[2,24,2304]{2,1,0:T(8,128)(2,1)S(1)}, u32[]{:S(2)}, u32[]{:S(2)}) collective-permute-start(bf16[2,24,2304]{2,1,0:T(8,128)(2,1)S(1)} %slice.302), channel_id=1, source_target_pairs={{0,16},{8,24},{16,0},{24,8},{1,17},{9,25},{17,1},{25,9},{2,18},{10... | collective-permute-start | bytes 663560 | tf_op jit(solution)/shard_map/ppermute | solution.py:643
  223.0 31.7 %collective-permute-start.33 = (bf16[256,768]{1,0:T(8,128)(2,1)S(1)}, bf16[256,768]{1,0:T(8,128)(2,1)S(1)}, u32[]{:S(2)}, u32[]{:S(2)}) collective-permute-start(bf16[256,768]{1,0:T(8,128)(2,1)S(1)} %fusion.10), channel_id=1, source_target_pairs={{0,4},{4,0},{1,5},{5,1},{2,6},{6,2},{3,7},{7,3},{8,12},{12,8},{9,1... | collective-permute-start | bytes 1179656 | tf_op jit(solution)/shard_map/ppermute | solution.py:590
  255.8 24.2 %collective-permute-start.36 = (bf16[256,768]{1,0:T(8,128)(2,1)}, bf16[256,768]{1,0:T(8,128)(2,1)}, u32[]{:S(2)}, u32[]{:S(2)}) collective-permute-start(bf16[256,768]{1,0:T(8,128)(2,1)} %add_convert_fusion.3), channel_id=1, source_target_pairs={{8,0},{16,8},{24,16},{0,24},{9,1},{17,9},{25,17},{1,25},{10,2},{18... | collective-permute-start | bytes 1179656 | tf_op jit(solution)/shard_map/ppermute | solution.py:581
  259.6 20.4 %collective-permute-start.35 = (bf16[1,24,2304]{2,1,0:T(8,128)(2,1)S(1)}, bf16[1,24,2304]{2,1,0:T(8,128)(2,1)}, u32[]{:S(2)}, u32[]{:S(2)}) collective-permute-start(bf16[1,24,2304]{2,1,0:T(8,128)(2,1)S(1)} %slice.303), channel_id=1, source_target_pairs={{0,8},{8,0},{16,24},{24,16},{1,9},{9,1},{17,25},{25,17},{2,10},{10... | collective-permute-start | bytes 331784 | tf_op jit(solution)/shard_map/ppermute | solution.py:643
  261.1 18.8 %collective-permute-start.37 = (bf16[256,768]{1,0:T(8,128)(2,1)}, bf16[256,768]{1,0:T(8,128)(2,1)}, u32[]{:S(2)}, u32[]{:S(2)}) collective-permute-start(bf16[256,768]{1,0:T(8,128)(2,1)} %fusion.11), channel_id=1, source_target_pairs={{0,4},{4,0},{1,5},{5,1},{2,6},{6,2},{3,7},{7,3},{8,12},{12,8},{9,1... | collective-permute-start | bytes 1179656 | tf_op jit(solution)/shard_map/ppermute | solution.py:590
  278.4 13.8 %collective-permute-start.38 = (bf16[4,4,24,640]{3,2,1,0:T(8,128)(2,1)S(1)}, bf16[4,4,24,640]{3,2,1,0:T(8,128)(2,1)S(1)}, u32[]{:S(2)}, u32[]{:S(2)}) collective-permute-start(bf16[4,4,24,640]{3,2,1,0:T(8,128)(2,1)S(1)} %get-tuple-element.406), channel_id=1, source_target_pairs={{1,0},{0,1},{3,2},{2,3},{5,4},{4,5},{7,6},{6,7},{9,8},{8,9},{11,10... | collective-permute-start | bytes 1474568 | tf_op jit(solution)/shard_map/ppermute | solution.py:581
  280.0 16.7 %collective-permute-start.40 = (bf16[2,256,768]{2,1,0:T(8,128)(2,1)S(1)}, bf16[2,256,768]{2,1,0:T(8,128)(2,1)S(1)}, u32[]{:S(2)}, u32[]{:S(2)}) collective-permute-start(bf16[2,256,768]{2,1,0:T(8,128)(2,1)S(1)} %get-tuple-element.369), channel_id=1, source_target_pairs={{0,2},{2,0},{1,3},{3,1},{4,6},{6,4},{5,7},{7,5},{8,10},{10,8},{9,1... | collective-permute-start | bytes 2359304 | tf_op jit(solution)/shard_map/ppermute | solution.py:588
  281.2 15.4 %collective-permute-start.39 = (bf16[256,768]{1,0:T(8,128)(2,1)S(1)}, bf16[256,768]{1,0:T(8,128)(2,1)S(1)}, u32[]{:S(2)}, u32[]{:S(2)}) collective-permute-start(bf16[256,768]{1,0:T(8,128)(2,1)S(1)} %add_convert_fusion.2), channel_id=1, source_target_pairs={{24,0},{0,8},{8,16},{16,24},{25,1},{1,9},{9,17},{17,25},{26,2},{2,... | collective-permute-start | bytes 1179656 | tf_op jit(solution)/shard_map/ppermute | solution.py:581
  296.9 13.0 %collective-permute-start.44 = (bf16[256,768]{1,0:T(8,128)(2,1)S(1)}, bf16[256,768]{1,0:T(8,128)(2,1)S(1)}, u32[]{:S(2)}, u32[]{:S(2)}) collective-permute-start(bf16[256,768]{1,0:T(8,128)(2,1)S(1)} %fusion.12), channel_id=1, source_target_pairs={{0,4},{4,0},{1,5},{5,1},{2,6},{6,2},{3,7},{7,3},{8,12},{12,8},{9,1... | collective-permute-start | bytes 1179656 | tf_op jit(solution)/shard_map/ppermute | solution.py:590
  297.3 12.5 %collective-permute-start.42 = (bf16[4,24,640]{2,1,0:T(8,128)(2,1)S(1)}, bf16[4,24,640]{2,1,0:T(8,128)(2,1)S(1)}, u32[]{:S(2)}, u32[]{:S(2)}) collective-permute-start(bf16[4,24,640]{2,1,0:T(8,128)(2,1)S(1)} %get-tuple-element.404), channel_id=1, source_target_pairs={{16,0},{24,8},{0,16},{8,24},{17,1},{25,9},{1,17},{9,25},{18,2},{26... | collective-permute-start | bytes 368648 | tf_op jit(solution)/shard_map/ppermute | solution.py:581
  297.4 12.5 %collective-permute-start.43 = (bf16[4,24,640]{2,1,0:T(8,128)(2,1)S(1)}, bf16[4,24,640]{2,1,0:T(8,128)(2,1)S(1)}, u32[]{:S(2)}, u32[]{:S(2)}) collective-permute-start(bf16[4,24,640]{2,1,0:T(8,128)(2,1)S(1)} %get-tuple-element.403), channel_id=1, source_target_pairs={{8,0},{16,8},{24,16},{0,24},{9,1},{17,9},{25,17},{1,25},{10,2},{18... | collective-permute-start | bytes 368648 | tf_op jit(solution)/shard_map/ppermute | solution.py:581
  (58 other events, 340.7 us)
Sparse Core Ops, SparseCore 0:
  11.4 107.0 all-gather.1
  164.6 144.4 reduce-scatter.1

commit v2 on v1

--- a/solution.py
+++ b/solution.py
@@ -636,15 +636,15 @@
         total = own_b(keep, got, 0) + sum(v.astype(f32) for v in more)
         return total[0], *away_sum(total, "x", 2)
 
-    def halve(half):
+    def halve(step):
         def over_q(own, got):
             total = own + got.astype(f32)
-            pairs = [(i, i ^ half) for i in range(n_q)]
-            return total[:half], lax.ppermute(total[half:].astype(bf16), "q", pairs)
+            pairs = [(i, i ^ step) for i in range(n_q)]
+            return total[0::2], lax.ppermute(total[1::2].astype(bf16), "q", pairs)
 
         return over_q
 
-    halves = [n_q >> (k + 1) for k in range(n_q.bit_length() - 1)]
+    halves = [1 << k for k in range(n_q.bit_length() - 1)]
     return Chain((keep, send), over_core, over_b, over_x, *[halve(half) for half in halves])
 
 

time: 333 us -> 332 us (level)
    ppermute x2, waiting for transfers between devices: 18.7 us -> 10 us  [over_q(): return (total[0::2], lax.ppermute(total[1::2].astype(bf16), 'q', pairs))]
    reduce_scatter x1, waiting for transfers between devices: 0.01 us -> 4.49 us  [per_device(): lax.psum_scatter(summands[-1], AXES, scatter_dimension=0, tiled=True)]
    ppermute x12, starting transfers between devices: 13.9 us -> 18.1 us  [square_swap(): return lax.ppermute(value, 'x', [(0, 1), (1, 0)])]
    unnamed x83 -> x81, local copies, waits for them, and re-layouts: 8.27 us -> 8.76 us
  transfers between devices with their start and end apart: 50 -> 50, of which waited for: 23 -> 23; matrix products, arithmetic and copies ran while one was open for 9% -> 9% of each run, Pallas kernels for 25% -> 26%
where the time goes in v2:
time: 332 us; the launch traced here: 328 us
  waiting for transfers between devices  106 us (32%)
  Pallas kernels  103 us (31%)
  starting transfers between devices  56.5 us (17%)
  local copies, waits for them, and re-layouts  26.9 us (8%)
  other arithmetic  18.6 us (6%)
  between operations  16.6 us (5%)
    ppermute x16, waiting for transfers between devices, from_shift(): lax.ppermute(value, axis, [((i + step) % count, i) for i in range(count)])  68.4 us
    pallas_call x4, Pallas kernels, attend_back_chunk(): pl.pallas_call(partial(backward_kernel, first, last, min(256, rows), min(...  47.2 us
    pallas_call x4, Pallas kernels, attend_chunk(): pl.pallas_call(partial(forward_kernel, first, last, min(1024, rows), min(...  36.1 us
    ppermute x16, starting transfers between devices, from_shift(): lax.ppermute(value, axis, [((i + step) % count, i) for i in range(count)])  30.1 us
    pallas_call x1, Pallas kernels, ffn_block(): pl.pallas_call(partial(ffn_kernel, layout), out_shape=out_shape + targets...  18.8 us
    ppermute x12, starting transfers between devices, square_swap(): return lax.ppermute(value, 'x', [(0, 1), (1, 0)])  18.1 us
    ppermute x12, waiting for transfers between devices, square_swap(): return lax.ppermute(value, 'x', [(0, 1), (1, 0)])  13.3 us
    ppermute x2, waiting for transfers between devices, over_q(): return (total[0::2], lax.ppermute(total[1::2].astype(bf16), 'q', pairs))  10 us
  transfers between devices with their start and end apart: 50, of which 23 were waited for; matrix products, arithmetic and copies ran while one was open for 9% of the time, Pallas kernels for 26%

profile of v2, /device:TPU:0, one launch (start us, length us, event | category | flops | bytes accessed | tf_op | source)
XLA Modules:
  0.0 327.8 jit_solution(9478283144160887121)
XLA Ops:
  10.1 3.0 collective-permute-start
  13.1 3.6 %collective-permute-start.1 = (bf16[256,768]{1,0:T(8,128)(2,1)S(1)}, bf16[256,768]{1,0:T(8,128)(2,1)}, u32[]{:S(2)}, u32[]{:S(2)}) collective-permute-start(bf16[256,768]{1,0:T(8,128)(2,1)S(1)} %bitcast.208), channel_id=1, source_target_pairs={{8,0},{16,8},{24,16},{0,24},{9,1},{17,9},{25,17},{1,25},{10,2},{18... | collective-permute-start | bytes 1179656 | tf_op jit(solution)/shard_map/ppermute | solution.py:581
  20.7 2.4 collective-permute-done.3
  23.3 4.0 %collective-permute-done.1.refs_1_.refs_3_ = bf16[256,768]{1,0:T(8,128)(2,1)} collective-permute-done((bf16[256,768]{1,0:T(8,128)(2,1)S(1)}, bf16[256,768]{1,0:T(8,128)(2,1)}, u32[]{:S(2)}, u32[]{:S(2)}) %collective-permute-start.1) | collective-permute-done | bytes 393248 | tf_op jit(solution)/shard_map/ppermute | solution.py:581
  27.6 4.4 %collective-permute-start.7 = (bf16[4,24,640]{2,1,0:T(8,128)(2,1)S(1)}, bf16[4,24,640]{2,1,0:T(8,128)(2,1)S(1)}, u32[]{:S(2)}, u32[]{:S(2)}) collective-permute-start(bf16[4,24,640]{2,1,0:T(8,128)(2,1)S(1)} %pad_maximum_fusion.8), channel_id=1, source_target_pairs={{8,0},{16,8},{24,16},{0,24},{9,1},{17,9},{25,17},{1,25},{10,2},{18... | collective-permute-start | bytes 368648 | tf_op jit(solution)/shard_map/ppermute | solution.py:581
  33.6 5.4 %collective-permute-done.7 = bf16[4,24,640]{2,1,0:T(8,128)(2,1)S(1)} collective-permute-done((bf16[4,24,640]{2,1,0:T(8,128)(2,1)S(1)}, bf16[4,24,640]{2,1,0:T(8,128)(2,1)S(1)}, u32[]{:S(2)}, u32[]{:S(2)}) %collective-permute-start.7) | collective-permute-done | bytes 122912 | tf_op jit(solution)/shard_map/ppermute | solution.py:581
  39.0 5.6 %collective-permute-done.8 = bf16[4,24,640]{2,1,0:T(8,128)(2,1)S(1)} collective-permute-done((bf16[4,24,640]{2,1,0:T(8,128)(2,1)S(1)}, bf16[4,24,640]{2,1,0:T(8,128)(2,1)S(1)}, u32[]{:S(2)}, u32[]{:S(2)}) %collective-permute-start.8) | collective-permute-done | bytes 122912 | tf_op jit(solution)/shard_map/ppermute | solution.py:581
  50.1 19.3 %collective-permute-done.11.refs_1_.refs_3_ = bf16[256,768]{1,0:T(8,128)(2,1)} collective-permute-done((bf16[256,768]{1,0:T(8,128)(2,1)S(1)}, bf16[256,768]{1,0:T(8,128)(2,1)}, u32[]{:S(2)}, u32[]{:S(2)}) %collective-permute-start.11) | collective-permute-done | bytes 393248 | tf_op jit(solution)/shard_map/ppermute | solution.py:581
  70.5 5.8 %collective-permute-start.14 = (bf16[256,768]{1,0:T(8,128)(2,1)}, bf16[256,768]{1,0:T(8,128)(2,1)}, u32[]{:S(2)}, u32[]{:S(2)}) collective-permute-start(bf16[256,768]{1,0:T(8,128)(2,1)} %collective-permute-done.1.refs_1_.refs_3_), channel_id=1, source_target_pairs={{8,0},{16,8},{24,16},{0,24},{9,1},{17,9},{25,17},{1,25},{10,2},{18... | collective-permute-start | bytes 1179656 | tf_op jit(solution)/shard_map/ppermute | solution.py:581
  78.1 8.6 %attend_forward.4 = (bf16[3,1024,256]{2,1,0:T(8,128)(2,1)}, bf16[3,1024,128]{2,1,0:T(8,128)(2,1)}, bf16[3,1024,256]{2,1,0:T(8,128)(2,1)S(1)}, bf16[3,1024,128]{2...) custom-call(s32[5]{0:T(128)S(1)} %stack.273.refs_0_, bf16[256,768]{1,0:T(8,128)(2,1)} %bitcast.205, ...), custom_call_target="tpu_custom_call" | custom-call | flops 8000000000 | bytes 10000000 | tf_op jit(solution)/shard_map/attend_forward/pallas_call | solution.py:190
  88.6 4.8 %collective-permute-done.14.refs_1_.refs_3_ = bf16[256,768]{1,0:T(8,128)(2,1)} collective-permute-done((bf16[256,768]{1,0:T(8,128)(2,1)}, bf16[256,768]{1,0:T(8,128)(2,1)}, u32[]{:S(2)}, u32[]{:S(2)}) %collective-permute-start.14) | collective-permute-done | bytes 393248 | tf_op jit(solution)/shard_map/ppermute | solution.py:581
  96.8 9.2 %attend_forward.5 = (bf16[3,1024,256]{2,1,0:T(8,128)(2,1)}, bf16[3,1024,128]{2,1,0:T(8,128)(2,1)}, f32[3,8,1024]{2,1,0:T(8,128)S(1)}, f32[3,80,1024]{2,1,0:T(8,128)S(1)}) custom-call(s32[5]{0:T(128)S(1)} %stack.240.refs_0_, bf16[256,768]{1,0:T(8,128)(2,1)} %collective-permute-done.1.refs_1_.refs_3_, bf16[256,768]{1,0:T(8,128)(2,1)} %get-tuple-element.219.refs_2_.refs_4_, ...), custom_call_target="tpu_custom_call" | custom-call | flops 8000000000 | bytes 10000000 | tf_op jit(solution)/shard_map/attend_forward/pallas_call | solution.py:190
  110.8 9.2 %attend_forward.6 = (bf16[3,1024,256]{2,1,0:T(8,128)(2,1)}, bf16[3,1024,128]{2,1,0:T(8,128)(2,1)}, f32[3,8,1024]{2,1,0:T(8,128)S(1)}, f32[3,80,1024]{2,1,0:T(8,128)S(1)}) custom-call(s32[5]{0:T(128)S(1)} %stack.235.refs_0_, bf16[256,768]{1,0:T(8,128)(2,1)} %collective-permute-done.11.refs_1_.refs_3_, bf16[256,768]{1,0:T(8,128)(2,1)} %get-tuple-element.247.refs_2_.refs_4_, ...), custom_call_target="tpu_custom_call" | custom-call | flops 8000000000 | bytes 10000000 | tf_op jit(solution)/shard_map/attend_forward/pallas_call | solution.py:190
  122.3 9.1 %attend_forward.7 = (bf16[3,1024,256]{2,1,0:T(8,128)(2,1)}, bf16[3,1024,128]{2,1,0:T(8,128)(2,1)}, bf16[256,192]{1,0:T(8,128)(2,1)S(1)}, bf16[256,192]{1,0:T(8,1...) custom-call(s32[5]{0:T(128)S(1)} %stack.230.refs_0_, ...), custom_call_target="tpu_custom_call" | custom-call | flops 8000000000 | bytes 10000000 | tf_op jit(solution)/shard_map/attend_forward/pallas_call | solution.py:190
  136.3 3.9 %collective-permute-done.18.refs_2_ = bf16[256,192]{1,0:T(8,128)(2,1)S(1)} collective-permute-done((bf16[256,192]{1,0:T(8,128)(2,1)S(1)}, bf16[256,192]{1,0:T(8,128)(2,1)S(1)}, u32[]{:S(2)}, u32[]{:S(2)}) %collective-permute-start.18) | collective-permute-done | bytes 98336 | tf_op jit(solution)/shard_map/ppermute | solution.py:588
  143.2 18.8 %feed_forward.1 = (bf16[256,768]{1,0:T(8,128)(2,1)}, f32[256,768]{1,0:T(8,128)S(1)}, bf16[256,192]{1,0:T(8,128)(2,1)S(1)}, bf16[256,192]{1,0:T(8,128)(2,1)S(1)},...) custom-call(s32[7]{0:T(128)S(1)} %stack.225.refs_0_, ...), custom_call_target="tpu_custom_call" | custom-call | flops 20000000000 | bytes 30000000 | tf_op jit(solution)/shard_map/feed_forward/pallas_call | solution.py:534
  165.8 3.2 collective-permute-done.23.refs_11_
  175.1 11.9 %attend_backward.4 = (bf16[2,256,768]{2,1,0:T(8,128)(2,1)S(1)}, bf16[2,256,768]{2,1,0:T(8,128)(2,1)S(1)}, bf16[3,1024,128]{2,1,0:T(8,128)(2,1)S(1)}, f32[3,64,10...) custom-call(bf16[3,1024,256]{2,1,0:T(8,128)(2,1)} %get-tuple-element.279.refs_0_, ...), custom_call_target="tpu_custom_call" | custom-call | flops 15000000512 | bytes 10000000 | tf_op jit(solution)/shard_map/attend_backward/pallas_call | solution.py:356
  187.0 7.3 %collective-permute-done.26 = bf16[2,4,24,2304]{3,2,1,0:T(8,128)(2,1)S(1)} collective-permute-done((bf16[2,4,24,2304]{3,2,1,0:T(8,128)(2,1)S(1)}, bf16[2,4,24,2304]{3,2,1,0:T(8,128)(2,1)S(1)}, u32[]{:S(2)}, u32[]{:S(2)}) %collective-permute-start.26) | collective-permute-done | bytes 884768 | tf_op jit(solution)/shard_map/ppermute | solution.py:581
  198.6 11.6 %attend_backward.5 = (bf16[2,256,768]{2,1,0:T(8,128)(2,1)S(1)}, bf16[2,256,768]{2,1,0:T(8,128)(2,1)S(1)}, f32[3,64,1024]{2,1,0:T(8,128)S(1)}, f32[768,512]{1,0:T(8,128)S(1)}, f32[8,512]{1,0:T(8,128)S(1)}) custom-call(bf16[3,1024,256]{2,1,0:T(8,128)(2,1)} %get-tuple-element.303.refs_0_, bf16[3,1024,128]{2,1,0:T(8,128)(2,1)} %get-tuple-element.304.refs_1_, ...), custom_call_target="tpu_custom_call" | custom-call | flops 15000000512 | bytes 10000000 | tf_op jit(solution)/shard_map/attend_backward/pallas_call | solution.py:356
  210.3 6.7 %collective-permute-done.29 = bf16[256,768]{1,0:T(8,128)(2,1)S(1)} collective-permute-done((bf16[256,768]{1,0:T(8,128)(2,1)S(1)}, bf16[256,768]{1,0:T(8,128)(2,1)S(1)}, u32[]{:S(2)}, u32[]{:S(2)}) %collective-permute-start.29) | collective-permute-done | bytes 393248 | tf_op jit(solution)/shard_map/ppermute | solution.py:590
  217.9 3.4 %collective-permute-start.31 = (bf16[2,24,2304]{2,1,0:T(8,128)(2,1)S(1)}, bf16[2,24,2304]{2,1,0:T(8,128)(2,1)S(1)}, u32[]{:S(2)}, u32[]{:S(2)}) collective-permute-start(bf16[2,24,2304]{2,1,0:T(8,128)(2,1)S(1)} %slice.192), channel_id=1, source_target_pairs={{0,8},{8,0},{16,24},{24,16},{1,9},{9,1},{17,25},{25,17},{2,10},{10... | collective-permute-start | bytes 663560 | tf_op jit(solution)/shard_map/ppermute | solution.py:643
  223.4 11.4 %attend_backward.6 = (bf16[2,256,768]{2,1,0:T(8,128)(2,1)S(1)}, bf16[2,256,768]{2,1,0:T(8,128)(2,1)S(1)}, f32[3,64,1024]{2,1,0:T(8,128)S(1)}, f32[768,512]{1,0:T(8,128)S(1)}, f32[8,512]{1,0:T(8,128)S(1)}) custom-call(bf16[3,1024,256]{2,1,0:T(8,128)(2,1)} %get-tuple-element.301.refs_0_, bf16[3,1024,128]{2,1,0:T(8,128)(2,1)} %get-tuple-element.302.refs_1_, ...), custom_call_target="tpu_custom_call" | custom-call | flops 15000000512 | bytes 10000000 | tf_op jit(solution)/shard_map/attend_backward/pallas_call | solution.py:356
  234.9 10.0 %collective-permute-done.31 = bf16[2,24,2304]{2,1,0:T(8,128)(2,1)S(1)} collective-permute-done((bf16[2,24,2304]{2,1,0:T(8,128)(2,1)S(1)}, bf16[2,24,2304]{2,1,0:T(8,128)(2,1)S(1)}, u32[]{:S(2)}, u32[]{:S(2)}) %collective-permute-start.31) | collective-permute-done | bytes 221216 | tf_op jit(solution)/shard_map/ppermute | solution.py:643
  246.0 2.6 collective-permute-start.36
  250.3 5.8 %collective-permute-start.37 = (bf16[256,768]{1,0:T(8,128)(2,1)}, bf16[256,768]{1,0:T(8,128)(2,1)}, u32[]{:S(2)}, u32[]{:S(2)}) collective-permute-start(bf16[256,768]{1,0:T(8,128)(2,1)} %fusion.11), channel_id=1, source_target_pairs={{0,4},{4,0},{1,5},{5,1},{2,6},{6,2},{3,7},{7,3},{8,12},{12,8},{9,1... | collective-permute-start | bytes 1179656 | tf_op jit(solution)/shard_map/ppermute | solution.py:590
  256.2 12.3 %attend_backward.7 = (bf16[2,256,768]{2,1,0:T(8,128)(2,1)S(1)}, bf16[2,256,768]{2,1,0:T(8,128)(2,1)S(1)}, bf16[768,640]{1,0:T(8,128)(2,1)S(1)}, f32[8,640]{1,0:T(8,128)S(1)}) custom-call(bf16[3,1024,256]{2,1,0:T(8,128)(2,1)} %get-tuple-element.275.refs_0_, bf16[3,1024,128]{2,1,0:T(8,128)(2,1)} %get-tuple-element.276.refs_1_, bf16[768,640]{1,0:T(8,128)(2,1)} %copy-done, ...), custom_call_target="tpu_custom_call" | custom-call | flops 15000000512 | bytes 10000000 | tf_op jit(solution)/shard_map/attend_backward/pallas_call | solution.py:356
  275.3 13.5 %collective-permute-done.38 = bf16[4,4,24,640]{3,2,1,0:T(8,128)(2,1)S(1)} collective-permute-done((bf16[4,4,24,640]{3,2,1,0:T(8,128)(2,1)S(1)}, bf16[4,4,24,640]{3,2,1,0:T(8,128)(2,1)S(1)}, u32[]{:S(2)}, u32[]{:S(2)}) %collective-permute-start.38) | collective-permute-done | bytes 491552 | tf_op jit(solution)/shard_map/ppermute | solution.py:581
  293.7 2.8 collective-permute-start.43
  296.6 2.4 collective-permute-done.41
  299.0 5.5 %collective-permute-done.42 = bf16[4,24,640]{2,1,0:T(8,128)(2,1)S(1)} collective-permute-done((bf16[4,24,640]{2,1,0:T(8,128)(2,1)S(1)}, bf16[4,24,640]{2,1,0:T(8,128)(2,1)S(1)}, u32[]{:S(2)}, u32[]{:S(2)}) %collective-permute-start.42) | collective-permute-done | bytes 122912 | tf_op jit(solution)/shard_map/ppermute | solution.py:581
  309.0 4.5 %reduce-scatter.2.cloned.1.call-done = bf16[24,4608]{1,0:T(8,128)(2,1)} async-done(((bf16[768,4608]{1,0:T(8,128)(2,1)}), bf16[24,4608]{1,0:T(8,128)(2,1)}) %reduce-scatter.2.cloned.1.call-update) | async-done | bytes 221200 | tf_op jit(solution)/shard_map/reduce_scatter | solution.py:841
  (294 shorter events, 78.9 us)
Async XLA Ops:
  7.2 126.8 %all-gather.2.cloned.1.call-start = ((), (), s32[]{:S(2)}) async-start(), calls=%async_computation.1 | async-start | bytes 5640192 | tf_op jit(solution)/shard_map/all_gather | solution.py:722
  10.0 303.4 %reduce-scatter.2.cloned.1.call-start = ((), (), s32[]{:S(2)}) async-start(), calls=%async_computation.2 | async-start | bytes 7299072 | tf_op jit(solution)/shard_map/reduce_scatter | solution.py:841
  10.1 13.2 %collective-permute-start = (bf16[256,768]{1,0:T(8,128)(2,1)S(1)}, bf16[256,768]{1,0:T(8,128)(2,1)S(1)}, u32[]{:S(2)}, u32[]{:S(2)}) collective-permute-start(bf16[256,768]{1,0:T(8,128)(2,1)S(1)} %bitcast.207), channel_id=1, source_target_pairs={{0,4},{4,0},{1,5},{5,1},{2,6},{6,2},{3,7},{7,3},{8,12},{12,8},{9,1... | collective-permute-start | bytes 1179656 | tf_op jit(solution)/shard_map/ppermute | solution.py:590
  13.1 14.2 %collective-permute-start.1 = (bf16[256,768]{1,0:T(8,128)(2,1)S(1)}, bf16[256,768]{1,0:T(8,128)(2,1)}, u32[]{:S(2)}, u32[]{:S(2)}) collective-permute-start(bf16[256,768]{1,0:T(8,128)(2,1)S(1)} %bitcast.208), channel_id=1, source_target_pairs={{8,0},{16,8},{24,16},{0,24},{9,1},{17,9},{25,17},{1,25},{10,2},{18... | collective-permute-start | bytes 1179656 | tf_op jit(solution)/shard_map/ppermute | solution.py:581
  27.5 17.2 %collective-permute-start.6 = (bf16[256,768]{1,0:T(8,128)(2,1)}, bf16[256,768]{1,0:T(8,128)(2,1)S(1)}, u32[]{:S(2)}, u32[]{:S(2)}) collective-permute-start(bf16[256,768]{1,0:T(8,128)(2,1)} %collective-permute-done.1.refs_1_.refs_3_), channel_id=1, source_target_pairs={{0,4},{4,0},{1,5},{5,1},{2,6},{6,2},{3,7},{7,3},{8,12},{12,8},{9,1... | collective-permute-start | bytes 1179656 | tf_op jit(solution)/shard_map/ppermute | solution.py:590
  27.6 11.5 %collective-permute-start.7 = (bf16[4,24,640]{2,1,0:T(8,128)(2,1)S(1)}, bf16[4,24,640]{2,1,0:T(8,128)(2,1)S(1)}, u32[]{:S(2)}, u32[]{:S(2)}) collective-permute-start(bf16[4,24,640]{2,1,0:T(8,128)(2,1)S(1)} %pad_maximum_fusion.8), channel_id=1, source_target_pairs={{8,0},{16,8},{24,16},{0,24},{9,1},{17,9},{25,17},{1,25},{10,2},{18... | collective-permute-start | bytes 368648 | tf_op jit(solution)/shard_map/ppermute | solution.py:581
  32.0 12.6 %collective-permute-start.8 = (bf16[4,24,640]{2,1,0:T(8,128)(2,1)S(1)}, bf16[4,24,640]{2,1,0:T(8,128)(2,1)S(1)}, u32[]{:S(2)}, u32[]{:S(2)}) collective-permute-start(bf16[4,24,640]{2,1,0:T(8,128)(2,1)S(1)} %pad_maximum_fusion.8), channel_id=1, source_target_pairs={{16,0},{24,8},{0,16},{8,24},{17,1},{25,9},{1,17},{9,25},{18,2},{26... | collective-permute-start | bytes 368648 | tf_op jit(solution)/shard_map/ppermute | solution.py:581
  32.0 12.6 %collective-permute-start.9 = (bf16[4,24,640]{2,1,0:T(8,128)(2,1)S(1)}, bf16[4,24,640]{2,1,0:T(8,128)(2,1)S(1)}, u32[]{:S(2)}, u32[]{:S(2)}) collective-permute-start(bf16[4,24,640]{2,1,0:T(8,128)(2,1)S(1)} %pad_maximum_fusion.8), channel_id=1, source_target_pairs={{24,0},{0,8},{8,16},{16,24},{25,1},{1,9},{9,17},{17,25},{26,2},{2,... | collective-permute-start | bytes 368648 | tf_op jit(solution)/shard_map/ppermute | solution.py:581
  46.0 23.4 %collective-permute-start.12 = (bf16[4,4,24,640]{3,2,1,0:T(8,128)(2,1)S(1)}, bf16[4,4,24,640]{3,2,1,0:T(8,128)(2,1)S(1)}, u32[]{:S(2)}, u32[]{:S(2)}) collective-permute-start(bf16[4,4,24,640]{3,2,1,0:T(8,128)(2,1)S(1)} %pad_maximum_fusion.5), channel_id=1, source_target_pairs={{1,0},{0,1},{3,2},{2,3},{5,4},{4,5},{7,6},{6,7},{9,8},{8,9},{11,10... | collective-permute-start | bytes 1474568 | tf_op jit(solution)/shard_map/ppermute | solution.py:581
  47.6 21.9 %collective-permute-start.11 = (bf16[256,768]{1,0:T(8,128)(2,1)S(1)}, bf16[256,768]{1,0:T(8,128)(2,1)}, u32[]{:S(2)}, u32[]{:S(2)}) collective-permute-start(bf16[256,768]{1,0:T(8,128)(2,1)S(1)} %bitcast.209), channel_id=1, source_target_pairs={{24,0},{0,8},{8,16},{16,24},{25,1},{1,9},{9,17},{17,25},{26,2},{2,... | collective-permute-start | bytes 1179656 | tf_op jit(solution)/shard_map/ppermute | solution.py:581
  69.5 23.9 %collective-permute-start.13 = (bf16[256,768]{1,0:T(8,128)(2,1)}, bf16[256,768]{1,0:T(8,128)(2,1)}, u32[]{:S(2)}, u32[]{:S(2)}) collective-permute-start(bf16[256,768]{1,0:T(8,128)(2,1)} %collective-permute-done.11.refs_1_.refs_3_), channel_id=1, source_target_pairs={{0,4},{4,0},{1,5},{5,1},{2,6},{6,2},{3,7},{7,3},{8,12},{12,8},{9,1... | collective-permute-start | bytes 1179656 | tf_op jit(solution)/shard_map/ppermute | solution.py:590
  70.5 22.8 %collective-permute-start.14 = (bf16[256,768]{1,0:T(8,128)(2,1)}, bf16[256,768]{1,0:T(8,128)(2,1)}, u32[]{:S(2)}, u32[]{:S(2)}) collective-permute-start(bf16[256,768]{1,0:T(8,128)(2,1)} %collective-permute-done.1.refs_1_.refs_3_), channel_id=1, source_target_pairs={{8,0},{16,8},{24,16},{0,24},{9,1},{17,9},{25,17},{1,25},{10,2},{18... | collective-permute-start | bytes 1179656 | tf_op jit(solution)/shard_map/ppermute | solution.py:581
  95.5 10.5 %collective-permute-start.15 = (bf16[2,256,768]{2,1,0:T(8,128)(2,1)}, bf16[2,256,768]{2,1,0:T(8,128)(2,1)}, u32[]{:S(2)}, u32[]{:S(2)}) collective-permute-start(bf16[2,256,768]{2,1,0:T(8,128)(2,1)} %pad_maximum_fusion.3), channel_id=1, source_target_pairs={{0,2},{2,0},{1,3},{3,1},{4,6},{6,4},{5,7},{7,5},{8,10},{10,8},{9,1... | collective-permute-start | bytes 2359304 | tf_op jit(solution)/shard_map/ppermute | solution.py:588
  95.6 12.5 %collective-permute-start.16 = (bf16[256,768]{1,0:T(8,128)(2,1)}, bf16[256,768]{1,0:T(8,128)(2,1)S(1)}, u32[]{:S(2)}, u32[]{:S(2)}) collective-permute-start(bf16[256,768]{1,0:T(8,128)(2,1)} %collective-permute-done.14.refs_1_.refs_3_), channel_id=1, source_target_pairs={{0,4},{4,0},{1,5},{5,1},{2,6},{6,2},{3,7},{7,3},{8,12},{12,8},{9,1... | collective-permute-start | bytes 1179656 | tf_op jit(solution)/shard_map/ppermute | solution.py:590
  110.2 9.9 %collective-permute-start.17 = (bf16[2,256,768]{2,1,0:T(8,128)(2,1)}, bf16[2,256,768]{2,1,0:T(8,128)(2,1)}, u32[]{:S(2)}, u32[]{:S(2)}) collective-permute-start(bf16[2,256,768]{2,1,0:T(8,128)(2,1)} %pad_maximum_fusion.4), channel_id=1, source_target_pairs={{0,2},{2,0},{1,3},{3,1},{4,6},{6,4},{5,7},{7,5},{8,10},{10,8},{9,1... | collective-permute-start | bytes 2359304 | tf_op jit(solution)/shard_map/ppermute | solution.py:588
  133.9 9.3 %collective-permute-start.21 = (bf16[384,6912]{1,0:T(8,128)(2,1)}, bf16[384,6912]{1,0:T(8,128)(2,1)}, u32[]{:S(2)}, u32[]{:S(2)}) collective-permute-start(bf16[384,6912]{1,0:T(8,128)(2,1)} %all-gather.2.cloned.1.call-done.refs_9_), channel_id=1, source_target_pairs={{0,2},{2,0},{1,3},{3,1},{4,6},{6,4},{5,7},{7,5},{8,10},{10,8},{9,1... | collective-permute-start | bytes 15925256 | tf_op jit(solution)/shard_map/ppermute | solution.py:588
  162.1 8.4 %collective-permute-start.25 = (bf16[2,4,48,2304]{3,2,1,0:T(8,128)(2,1)}, bf16[2,4,48,2304]{3,2,1,0:T(8,128)(2,1)}, u32[]{:S(2)}, u32[]{:S(2)}) collective-permute-start(bf16[2,4,48,2304]{3,2,1,0:T(8,128)(2,1)} %get-tuple-element.286), channel_id=1, source_target_pairs={{0,2},{2,0},{1,3},{3,1},{4,6},{6,4},{5,7},{7,5},{8,10},{10,8},{9,1... | collective-permute-start | bytes 5308424 | tf_op jit(solution)/shard_map/ppermute | solution.py:588
  172.2 22.1 %collective-permute-start.26 = (bf16[2,4,24,2304]{3,2,1,0:T(8,128)(2,1)S(1)}, bf16[2,4,24,2304]{3,2,1,0:T(8,128)(2,1)S(1)}, u32[]{:S(2)}, u32[]{:S(2)}) collective-permute-start(bf16[2,4,24,2304]{3,2,1,0:T(8,128)(2,1)S(1)} %fusion.4), channel_id=1, source_target_pairs={{1,0},{0,1},{3,2},{2,3},{5,4},{4,5},{7,6},{6,7},{9,8},{8,9},{11,10... | collective-permute-start | bytes 2654216 | tf_op jit(solution)/shard_map/ppermute | solution.py:581
  195.9 14.4 %collective-permute-start.28 = (bf16[4,24,2304]{2,1,0:T(8,128)(2,1)S(1)}, bf16[4,24,2304]{2,1,0:T(8,128)(2,1)S(1)}, u32[]{:S(2)}, u32[]{:S(2)}) collective-permute-start(bf16[4,24,2304]{2,1,0:T(8,128)(2,1)S(1)} %fusion.7), channel_id=1, source_target_pairs={{4,0},{0,4},{5,1},{1,5},{6,2},{2,6},{7,3},{3,7},{12,8},{8,12},{13,... | collective-permute-start | bytes 1327112 | tf_op jit(solution)/shard_map/ppermute | solution.py:581
  198.0 19.0 %collective-permute-start.29 = (bf16[256,768]{1,0:T(8,128)(2,1)S(1)}, bf16[256,768]{1,0:T(8,128)(2,1)S(1)}, u32[]{:S(2)}, u32[]{:S(2)}) collective-permute-start(bf16[256,768]{1,0:T(8,128)(2,1)S(1)} %fusion.9), channel_id=1, source_target_pairs={{0,4},{4,0},{1,5},{5,1},{2,6},{6,2},{3,7},{7,3},{8,12},{12,8},{9,1... | collective-permute-start | bytes 1179656 | tf_op jit(solution)/shard_map/ppermute | solution.py:590
  217.1 27.8 %collective-permute-start.32 = (bf16[256,768]{1,0:T(8,128)(2,1)S(1)}, bf16[256,768]{1,0:T(8,128)(2,1)S(1)}, u32[]{:S(2)}, u32[]{:S(2)}) collective-permute-start(bf16[256,768]{1,0:T(8,128)(2,1)S(1)} %add_convert_fusion.4), channel_id=1, source_target_pairs={{24,0},{0,8},{8,16},{16,24},{25,1},{1,9},{9,17},{17,25},{26,2},{2,... | collective-permute-start | bytes 1179656 | tf_op jit(solution)/shard_map/ppermute | solution.py:581
  217.9 27.0 %collective-permute-start.31 = (bf16[2,24,2304]{2,1,0:T(8,128)(2,1)S(1)}, bf16[2,24,2304]{2,1,0:T(8,128)(2,1)S(1)}, u32[]{:S(2)}, u32[]{:S(2)}) collective-permute-start(bf16[2,24,2304]{2,1,0:T(8,128)(2,1)S(1)} %slice.192), channel_id=1, source_target_pairs={{0,8},{8,0},{16,24},{24,16},{1,9},{9,1},{17,25},{25,17},{2,10},{10... | collective-permute-start | bytes 663560 | tf_op jit(solution)/shard_map/ppermute | solution.py:643
  221.6 23.3 %collective-permute-start.33 = (bf16[256,768]{1,0:T(8,128)(2,1)S(1)}, bf16[256,768]{1,0:T(8,128)(2,1)S(1)}, u32[]{:S(2)}, u32[]{:S(2)}) collective-permute-start(bf16[256,768]{1,0:T(8,128)(2,1)S(1)} %fusion.10), channel_id=1, source_target_pairs={{0,4},{4,0},{1,5},{5,1},{2,6},{6,2},{3,7},{7,3},{8,12},{12,8},{9,1... | collective-permute-start | bytes 1179656 | tf_op jit(solution)/shard_map/ppermute | solution.py:590
  246.0 25.8 %collective-permute-start.36 = (bf16[256,768]{1,0:T(8,128)(2,1)}, bf16[256,768]{1,0:T(8,128)(2,1)}, u32[]{:S(2)}, u32[]{:S(2)}) collective-permute-start(bf16[256,768]{1,0:T(8,128)(2,1)} %add_convert_fusion.3), channel_id=1, source_target_pairs={{8,0},{16,8},{24,16},{0,24},{9,1},{17,9},{25,17},{1,25},{10,2},{18... | collective-permute-start | bytes 1179656 | tf_op jit(solution)/shard_map/ppermute | solution.py:581
  248.6 23.1 %collective-permute-start.35 = (bf16[1,24,2304]{2,1,0:T(8,128)(2,1)S(1)}, bf16[1,24,2304]{2,1,0:T(8,128)(2,1)}, u32[]{:S(2)}, u32[]{:S(2)}) collective-permute-start(bf16[1,24,2304]{2,1,0:T(8,128)(2,1)S(1)} %slice.301), channel_id=1, source_target_pairs={{0,16},{8,24},{16,0},{24,8},{1,17},{9,25},{17,1},{25,9},{2,18},{10... | collective-permute-start | bytes 331784 | tf_op jit(solution)/shard_map/ppermute | solution.py:643
  250.3 21.4 %collective-permute-start.37 = (bf16[256,768]{1,0:T(8,128)(2,1)}, bf16[256,768]{1,0:T(8,128)(2,1)}, u32[]{:S(2)}, u32[]{:S(2)}) collective-permute-start(bf16[256,768]{1,0:T(8,128)(2,1)} %fusion.11), channel_id=1, source_target_pairs={{0,4},{4,0},{1,5},{5,1},{2,6},{6,2},{3,7},{7,3},{8,12},{12,8},{9,1... | collective-permute-start | bytes 1179656 | tf_op jit(solution)/shard_map/ppermute | solution.py:590
  271.5 17.4 %collective-permute-start.38 = (bf16[4,4,24,640]{3,2,1,0:T(8,128)(2,1)S(1)}, bf16[4,4,24,640]{3,2,1,0:T(8,128)(2,1)S(1)}, u32[]{:S(2)}, u32[]{:S(2)}) collective-permute-start(bf16[4,4,24,640]{3,2,1,0:T(8,128)(2,1)S(1)} %get-tuple-element.408), channel_id=1, source_target_pairs={{1,0},{0,1},{3,2},{2,3},{5,4},{4,5},{7,6},{6,7},{9,8},{8,9},{11,10... | collective-permute-start | bytes 1474568 | tf_op jit(solution)/shard_map/ppermute | solution.py:581
  271.8 17.6 %collective-permute-start.40 = (bf16[2,256,768]{2,1,0:T(8,128)(2,1)S(1)}, bf16[2,256,768]{2,1,0:T(8,128)(2,1)S(1)}, u32[]{:S(2)}, u32[]{:S(2)}) collective-permute-start(bf16[2,256,768]{2,1,0:T(8,128)(2,1)S(1)} %get-tuple-element.369), channel_id=1, source_target_pairs={{0,2},{2,0},{1,3},{3,1},{4,6},{6,4},{5,7},{7,5},{8,10},{10,8},{9,1... | collective-permute-start | bytes 2359304 | tf_op jit(solution)/shard_map/ppermute | solution.py:588
  273.5 15.8 %collective-permute-start.39 = (bf16[256,768]{1,0:T(8,128)(2,1)S(1)}, bf16[256,768]{1,0:T(8,128)(2,1)S(1)}, u32[]{:S(2)}, u32[]{:S(2)}) collective-permute-start(bf16[256,768]{1,0:T(8,128)(2,1)S(1)} %add_convert_fusion.2), channel_id=1, source_target_pairs={{24,0},{0,8},{8,16},{16,24},{25,1},{1,9},{9,17},{17,25},{26,2},{2,... | collective-permute-start | bytes 1179656 | tf_op jit(solution)/shard_map/ppermute | solution.py:581
  289.6 14.9 %collective-permute-start.44 = (bf16[256,768]{1,0:T(8,128)(2,1)S(1)}, bf16[256,768]{1,0:T(8,128)(2,1)S(1)}, u32[]{:S(2)}, u32[]{:S(2)}) collective-permute-start(bf16[256,768]{1,0:T(8,128)(2,1)S(1)} %fusion.12), channel_id=1, source_target_pairs={{0,4},{4,0},{1,5},{5,1},{2,6},{6,2},{3,7},{7,3},{8,12},{12,8},{9,1... | collective-permute-start | bytes 1179656 | tf_op jit(solution)/shard_map/ppermute | solution.py:590
  292.3 12.2 %collective-permute-start.42 = (bf16[4,24,640]{2,1,0:T(8,128)(2,1)S(1)}, bf16[4,24,640]{2,1,0:T(8,128)(2,1)S(1)}, u32[]{:S(2)}, u32[]{:S(2)}) collective-permute-start(bf16[4,24,640]{2,1,0:T(8,128)(2,1)S(1)} %get-tuple-element.406), channel_id=1, source_target_pairs={{16,0},{24,8},{0,16},{8,24},{17,1},{25,9},{1,17},{9,25},{18,2},{26... | collective-permute-start | bytes 368648 | tf_op jit(solution)/shard_map/ppermute | solution.py:581
  293.7 10.8 %collective-permute-start.43 = (bf16[4,24,640]{2,1,0:T(8,128)(2,1)S(1)}, bf16[4,24,640]{2,1,0:T(8,128)(2,1)S(1)}, u32[]{:S(2)}, u32[]{:S(2)}) collective-permute-start(bf16[4,24,640]{2,1,0:T(8,128)(2,1)S(1)} %get-tuple-element.405), channel_id=1, source_target_pairs={{8,0},{16,8},{24,16},{0,24},{9,1},{17,9},{25,17},{1,25},{10,2},{18... | collective-permute-start | bytes 368648 | tf_op jit(solution)/shard_map/ppermute | solution.py:581
  (56 other events, 310.2 us)
Sparse Core Ops, SparseCore 0:
  11.4 106.9 all-gather.1
  164.6 148.7 reduce-scatter.1
